TPU v7x, 256 devices: a whole 4x4x8 slice. The times are simulated.
256 devices in a mesh: gx: 32 (over y, x, core), gy: 8 (over z).
Axes of the slice: x: 4, y: 4, z: 8, core: 2. Of those that a mesh axis runs over, the one named last changes fastest.
Arguments:
- operator_blocks: float32 [64, 16, 12, 7, 64, 64], P('gx', 'gy'), may hold values from -1 to 13, as said below
- start_block: float32 [64, 16, 12, 64, 16], P('gx', 'gy'), may hold values from -4000 to 4000
Outputs:
- orthonormal: float32 [64, 16, 12, 64, 80], P('gx', 'gy')
- triangle: float32 [80, 80], replicated
Inputs may be any that keep to these rules, and one draw needn't show every extreme that they name: `operator_blocks`: the own block of every element is diagonally dominant; other entries are small.
All inputs are finite; a program needn't handle non-finite values.
Results may differ from a plain program's by a relative error of at most 0.0003.
Values sent between devices are 32-bit elements; how exact they have to be, the bound alone decides.
No kernel may reach another device: no remote copies, remote signals or barrier semaphores. Data moves between devices by JAX's collectives and lax.ppermute only.
A program may use at most 64 MiB of HBM per device.

v0:
```python
import functools

import jax
import jax.numpy as jnp
from jax import lax
from jax.experimental import pallas as pl
from jax.experimental.pallas import tpu as pltpu
from jax.sharding import PartitionSpec as P

F32 = jnp.float32
BF16 = jnp.bfloat16
Z = 12
R = 16
U = 64
L = 2 * U
FACE = Z * L
WIDE = 2 * FACE
STEPS = 4
COLS = (STEPS + 1) * R
VMEM_LIMIT = 16 * 1024 * 1024
NT = (((1,), (1,)), ((), ()))
TN = (((0,), (0,)), ((), ()))

VM = pl.BlockSpec(memory_space=pltpu.VMEM)


def low_lanes(shape):
    return lax.broadcasted_iota(jnp.int32, shape, len(shape) - 1) < U


def split(value):
    high = value.astype(BF16)
    return high, (value - high.astype(F32)).astype(BF16)


def product(left, w_high, w_low):
    high, low = split(left)
    both = lax.dot_general(
        jnp.concatenate([high, low], axis=0), w_high, NT, preferred_element_type=F32
    )
    rest = lax.dot_general(high, w_low, NT, preferred_element_type=F32)
    total = both[: 2 * R] + both[2 * R :] + rest
    return jnp.where(low_lanes((R, L)), total[:R], total[R:])


def swapped(pair):
    return pltpu.roll(pair, U, 1)


def parity():
    return lax.axis_index("gx") & 1, lax.axis_index("gy") & 1


def lanes(x, z):
    base = (x * Z + z) * L
    return slice(base, base + L)


def store_packets(pairs, px, py, e_ref, o_ref, ee_ref, oo_ref):
    low = low_lanes((R, L))
    for z in range(Z):
        at = slice(z * L, (z + 1) * L)
        first, second = pairs[0][z], pairs[1][z]
        e_ref[:, at] = jnp.where(px == 0, second, first)
        o_ref[:, at] = jnp.where(px == 0, first, second)
        face0 = jnp.where(low, first, swapped(second))
        face1 = jnp.where(low, swapped(first), second)
        ee_ref[:, at] = jnp.where(py == 0, face1, face0)
        oo_ref[:, at] = jnp.where(py == 0, face0, face1)


def begin_kernel(s_ref, p_ref, e_ref, o_ref, ee_ref, oo_ref):
    px, py = parity()
    pairs = [[None] * Z for _ in range(2)]
    for x in range(2):
        for z in range(Z):
            pair = jnp.concatenate([s_ref[x, 0, z], s_ref[x, 1, z]], axis=1)
            p_ref[:, lanes(x, z)] = pair
            pairs[x][z] = pair
    store_packets(pairs, px, py, e_ref, o_ref, ee_ref, oo_ref)


def weights_kernel(a_ref, lh_ref, ll_ref, eh_ref, el_ref):
    zero = jnp.zeros((U, U), F32)
    for x in range(2):
        for y in range(2):
            rows = slice(y * U, (y + 1) * U)
            f = lambda k: a_ref[x, y, 0, k]
            tiles = (
                (f(0), f(2 - x)),
                (f(5), f(6)),
                (f(4 - y), zero),
            )
            for t, (one, two) in enumerate(tiles):
                high, low = split(jnp.concatenate([one, two], axis=1))
                lh_ref[x, 0, rows, t * L : (t + 1) * L] = high
                ll_ref[x, 0, rows, t * L : (t + 1) * L] = low
            along_x, along_y = f(1 + x), f(3 + y)
            outer = (along_y, along_x) if x == 0 else (along_x, along_y)
            high, low = split(jnp.concatenate(outer, axis=1))
            eh_ref[x, 0, rows, :] = high
            el_ref[x, 0, rows, :] = low


def local_kernel(p_ref, lh_ref, ll_ref, out_ref):
    low = low_lanes((R, L))
    pairs = [[p_ref[:, lanes(x, z)] for z in range(Z)] for x in range(2)]
    turned = [[swapped(v) for v in row] for row in pairs]
    zero = jnp.zeros((R, L), F32)

    def at(rows, x, z):
        return rows[x][z] if 0 <= z < Z else zero

    for x in range(2):
        for z in range(Z):
            a = [
                jnp.where(low, pairs[x][z], turned[1 - x][z]),
                jnp.where(low, at(pairs, x, z - 1), at(turned, x, z + 1)),
                turned[x][z],
            ]
            b = [
                jnp.where(low, turned[x][z], pairs[1 - x][z]),
                jnp.where(low, at(turned, x, z - 1), at(pairs, x, z + 1)),
                pairs[x][z],
            ]
            left = jnp.concatenate([jnp.concatenate(a, axis=1), jnp.concatenate(b, axis=1)], axis=0)
            out_ref[:, lanes(x, z)] = product(left, lh_ref[x, z], ll_ref[x, z])


def outer_kernel(first, last, *refs):
    part_ref, p_ref = refs[:2]
    refs = refs[2:]
    if not first:
        before_ref, refs = refs[0], refs[1:]
    e_ref, o_ref, ee_ref, oo_ref, eh_ref, el_ref, *outs = refs
    px, py = parity()
    low = low_lanes((R, L))
    gx, gy = lax.axis_index("gx"), lax.axis_index("gy")
    o_there = jnp.logical_and(gx > 0, gx < lax.axis_size("gx") - 1)
    oo_there = jnp.logical_and(gy > 0, gy < lax.axis_size("gy") - 1)
    pairs = [[None] * Z for _ in range(2)]
    for z in range(Z):
        at = slice(z * L, (z + 1) * L)
        e, o, ee, oo = e_ref[:, at], o_ref[:, at], ee_ref[:, at], oo_ref[:, at]
        o = jnp.where(o_there, o, 0.0)
        oo = jnp.where(oo_there, oo, 0.0)
        x0, x1 = jnp.where(px == 0, o, e), jnp.where(px == 0, e, o)
        ym, yp = jnp.where(py == 0, oo, ee), jnp.where(py == 0, ee, oo)
        left0 = jnp.concatenate([jnp.where(low, ym, swapped(x0)), jnp.where(low, yp, x0)], axis=0)
        left1 = jnp.concatenate([jnp.where(low, x1, ym), jnp.where(low, swapped(x1), yp)], axis=0)
        for x, left in ((0, left0), (1, left1)):
            here = lanes(x, z)
            applied = part_ref[:, here] + product(left, eh_ref[x, z], el_ref[x, z])
            shifted = (applied - 8.0 * p_ref[:, here]) * (1.0 / 6.0)
            pairs[x][z] = shifted if first else 2.0 * shifted - before_ref[:, here]
            outs[0][:, here] = pairs[x][z]
    if not last:
        store_packets(pairs, px, py, *outs[1:])


def gram_kernel(*refs):
    *blocks, g_ref = refs
    tall = jnp.concatenate([b[...] for b in blocks], axis=0)
    g_ref[:, :COLS] = lax.dot_general(
        tall, tall, NT, precision=lax.Precision.HIGHEST, preferred_element_type=F32
    )
    g_ref[:, COLS:] = jnp.zeros((COLS, L - COLS), F32)


def finish_kernel(g_ref, b0, b1, b2, b3, b4, q_ref, r_ref):
    tiles = [g_ref[8 * i : 8 * i + 8, :] for i in range(COLS // 8)]
    lane = lax.broadcasted_iota(jnp.int32, (8, L), 1)
    sub = lax.broadcasted_iota(jnp.int32, (8, L), 0)
    pivots = []
    for k in range(COLS):
        t, s = divmod(k, 8)
        row = jnp.broadcast_to(tiles[t][s : s + 1, :], (8, L))
        pivot = jnp.broadcast_to(tiles[t][s : s + 1, k : k + 1], (8, L))
        pivots.append(pivot)
        scaled = row * (1.0 / pivot)
        here = lane == k
        scaled = jnp.where(here, 1.0 / pivot, scaled)
        for i in range(t, COLS // 8):
            column = jnp.broadcast_to(tiles[i][:, k : k + 1], (8, L))
            kept = jnp.where(here, 0.0, tiles[i])
            new = kept - column * scaled
            tiles[i] = new if i > t else jnp.where(sub > s, new, tiles[i])
    inverse = []
    for i in range(COLS // 8):
        pivot = pivots[8 * i]
        for s in range(1, 8):
            pivot = jnp.where(sub == s, pivots[8 * i + s], pivot)
        scale = lax.rsqrt(pivot)
        rows = tiles[i] * scale
        index = sub + 8 * i
        r_ref[8 * i : 8 * i + 8, :] = jnp.where(lane >= index, rows, 0.0)[:, :COLS]
        inverse.append(jnp.where(lane < index, rows, jnp.where(lane == index, scale, 0.0)))
    inverse = jnp.concatenate(inverse, axis=0)[:, :COLS]
    blocks = (b0, b1, b2, b3, b4)
    for x in range(2):
        for z in range(Z):
            tall = jnp.concatenate([b[:, lanes(x, z)] for b in blocks], axis=0)
            rows = jnp.transpose(
                jnp.dot(inverse, tall, precision=lax.Precision.HIGHEST, preferred_element_type=F32)
            )
            q_ref[x, 0, z] = rows[:U]
            q_ref[x, 1, z] = rows[U:]


def call(kernel, outs, n_in, **more):
    shapes = [jax.ShapeDtypeStruct(s, d) for s, d in outs]
    one = len(shapes) == 1
    return pl.pallas_call(
        kernel,
        out_shape=shapes[0] if one else shapes,
        in_specs=[VM] * n_in,
        out_specs=VM if one else [VM] * len(shapes),
        compiler_params=pltpu.CompilerParams(vmem_limit_bytes=VMEM_LIMIT),
        **more,
    )


PACKETS = [((R, FACE), F32)] * 4
BLOCK = [((R, WIDE), F32)]


def exchange(packets):
    wide = lax.axis_size("gx")
    deep = lax.axis_size("gy")

    def even(n):
        return [(i, i ^ 1) for i in range(n)]

    def odd(n):
        there = [(i, (i + 1) % n) for i in range(1, n, 2)]
        return there + [(j, i) for i, j in there]

    e, o, ee, oo = packets
    oo = lax.ppermute(oo, "gy", odd(deep))
    ee = lax.ppermute(ee, "gy", even(deep))
    o = lax.ppermute(o, "gx", odd(wide))
    e = lax.ppermute(e, "gx", even(wide))
    return e, o, ee, oo


def total_over_devices(gram):
    for axis, masks in (("gx", (1, 2, 6, 8, 24)), ("gy", (1, 2, 7))):
        count = lax.axis_size(axis)
        for mask in masks:
            gram = gram + lax.ppermute(gram, axis, [(i, i ^ mask) for i in range(count)])
    return gram


def weights(operator_blocks):
    local, outer = (2, Z, L, 3 * L), (2, Z, L, L)
    block = lambda width: pl.BlockSpec((2, 1, L, width), lambda z: (0, z, 0, 0))
    return pl.pallas_call(
        weights_kernel,
        grid=(Z,),
        out_shape=[jax.ShapeDtypeStruct(s, BF16) for s in (local, local, outer, outer)],
        in_specs=[pl.BlockSpec((2, 2, 1, 7, U, U), lambda z: (0, 0, z, 0, 0, 0))],
        out_specs=[block(3 * L), block(3 * L), block(L), block(L)],
        compiler_params=pltpu.CompilerParams(vmem_limit_bytes=VMEM_LIMIT),
    )(operator_blocks)


def per_device(operator_blocks, start_block):
    start = jnp.swapaxes(start_block, 3, 4)
    now, *packets = call(begin_kernel, BLOCK + PACKETS, 1)(start)
    arrived = exchange(packets)
    local_high, local_low, outer_high, outer_low = weights(operator_blocks)
    blocks = [now]
    for step in range(STEPS):
        first, last = step == 0, step == STEPS - 1
        part = call(local_kernel, BLOCK, 3)(blocks[-1], local_high, local_low)
        before = [] if first else [blocks[-2]]
        operands = [part, blocks[-1], *before, *arrived, outer_high, outer_low]
        outs = call(
            functools.partial(outer_kernel, first, last),
            BLOCK + ([] if last else PACKETS),
            len(operands),
        )(*operands)
        if last:
            blocks.append(outs)
        else:
            blocks.append(outs[0])
            arrived = exchange(outs[1:])
    gram = call(gram_kernel, [((COLS, L), F32)], len(blocks))(*blocks)
    gram = total_over_devices(gram)
    return call(finish_kernel, [((2, 2, Z, U, COLS), F32), ((COLS, COLS), F32)], 1 + len(blocks))(
        gram, *blocks
    )


def solution(mesh):
    in_specs = (P("gx", "gy", None, None, None, None), P("gx", "gy", None, None, None))
    out_specs = (P("gx", "gy", None, None, None), P())
    return jax.shard_map(
        per_device, mesh=mesh, in_specs=in_specs, out_specs=out_specs, check_vma=False
    )
```

profile of v0, /device:TPU:32, one launch (start us, length us, event | category | flops | bytes accessed | tf_op | source)
XLA Modules:
  0.0 100.5 jit_solution(7152844400735797146)
XLA Ops:
  0.6 1.0 copy-done.1
  1.6 0.2 shard_map.41
  1.8 0.1 collective-permute-start
  1.9 5.3 %collective-permute-start.1 = (f32[16,1536]{1,0:T(8,128)S(1)}, f32[16,1536]{1,0:T(8,128)S(1)}, u32[]{:S(2)}, u32[]{:S(2)}) collective-permute-start(f32[16,1536]{1,0:T(8,128)S(1)} %get-tuple-element.30), channel_id=1, source_target_pairs={{8,16},{24,32},{40,48},{56,64},{72,80},{88,96},{104,112},{120,128}... | collective-permute-start | bytes 294920 | tf_op jit(solution)/shard_map/ppermute | solution.py:241
  7.3 0.1 collective-permute-start.2
  7.4 3.7 %collective-permute-start.3 = (f32[16,1536]{1,0:T(8,128)S(1)}, f32[16,1536]{1,0:T(8,128)S(1)}, u32[]{:S(2)}, u32[]{:S(2)}) collective-permute-start(f32[16,1536]{1,0:T(8,128)S(1)} %get-tuple-element.32), channel_id=1, source_target_pairs={{1,2},{3,4},{5,6},{7,0},{2,1},{4,3},{6,5},{0,7},{9,10},{11,12},{13... | collective-permute-start | bytes 294920 | tf_op jit(solution)/shard_map/ppermute | solution.py:239
  11.1 4.1 %copy-done = f32[2,2,12,7,64,64]{5,4,3,2,1,0:T(8,128)S(1)} copy-done((f32[2,2,12,7,64,64]{5,4,3,2,1,0:T(8,128)S(1)}, f32[2,2,12,7,64,64]{5,4,3,2,1,0:T(8,128)}, u32[]{:S(2)}) %copy-start) | copy-done | bytes 5505048
  15.2 3.5 %shard_map.42 = (bf16[2,12,128,384]{3,2,1,0:T(8,128)(2,1)S(1)}, bf16[2,12,128,384]{3,2,1,0:T(8,128)(2,1)S(1)}, bf16[2,12,128,128]{3,2,1,0:T(8,128)(2,1)S(1)}, bf16[2,12,128,128]{3,2,1,0:T(8,128)(2,1)S(1)}) custom-call(f32[2,2,12,7,64,64]{5,4,3,2,1,0:T(8,128)S(1)} %copy-done), custom_call_target="tpu_custom_call" | custom-call | tf_op jit(solution)/shard_map/pallas_call | solution.py:257
  18.7 2.1 %shard_map.43.refs_0_ = f32[16,3072]{1,0:T(8,128)S(1)} custom-call(f32[16,3072]{1,0:T(8,128)S(1)} %get-tuple-element.26.p_ref.refs_1_.refs_2_.refs_0_.b0, bf16[2,12,128,384]{3,2,1,0:T(8,128)(2,1)S(1)} %get-tuple-element.27.lh_ref, bf16[2,12,128,384]{3,2,1,0:T(8,128)(2,1)S(1)} %get-tuple-element.28.ll_ref), custom_call_target="tpu_custom_call" | custom-call | tf_op jit(solution)/shard_map/pallas_call | solution.py:275
  20.8 1.2 %shard_map.44 = (f32[16,3072]{1,0:T(8,128)S(1)}, f32[16,1536]{1,0:T(8,128)S(1)}, f32[16,1536]{1,0:T(8,128)S(1)}, f32[16,1536]{1,0:T(8,128)S(1)}, f32[16,1536]{1,0:T(8,128)S(1)}) custom-call(f32[16,3072]{1,0:T(8,128)S(1)} %shard_map.43.refs_0_, f32[16,3072]{1,0:T(8,128)S(1)} %get-tuple-element.26.p_ref.refs_1_.refs_2_.refs_0_.b0, ...), custom_call_target="tpu_custom_call" | custom-call | tf_op jit(solution)/shard_map/pallas_call | solution.py:278
  22.0 0.1 collective-permute-start.4
  22.0 0.9 collective-permute-start.5
  23.0 3.1 %collective-permute-start.6 = (f32[16,1536]{1,0:T(8,128)S(1)}, f32[16,1536]{1,0:T(8,128)S(1)}, u32[]{:S(2)}, u32[]{:S(2)}) collective-permute-start(f32[16,1536]{1,0:T(8,128)S(1)} %get-tuple-element.38), channel_id=1, source_target_pairs={{0,1},{1,0},{2,3},{3,2},{4,5},{5,4},{6,7},{7,6},{8,9},{9,8},{10,11... | collective-permute-start | bytes 294920 | tf_op jit(solution)/shard_map/ppermute | solution.py:240
  26.1 1.0 %collective-permute-start.7 = (f32[16,1536]{1,0:T(8,128)S(1)}, f32[16,1536]{1,0:T(8,128)S(1)}, u32[]{:S(2)}, u32[]{:S(2)}) collective-permute-start(f32[16,1536]{1,0:T(8,128)S(1)} %get-tuple-element.39), channel_id=1, source_target_pairs={{1,2},{3,4},{5,6},{7,0},{2,1},{4,3},{6,5},{0,7},{9,10},{11,12},{13... | collective-permute-start | bytes 294920 | tf_op jit(solution)/shard_map/ppermute | solution.py:239
  27.1 2.0 %shard_map.45.refs_0_ = f32[16,3072]{1,0:T(8,128)S(1)} custom-call(f32[16,3072]{1,0:T(8,128)S(1)} %get-tuple-element.35.p_ref.refs_1_.refs_2_.b1, bf16[2,12,128,384]{3,2,1,0:T(8,128)(2,1)S(1)} %get-tuple-element.27.lh_ref, bf16[2,12,128,384]{3,2,1,0:T(8,128)(2,1)S(1)} %get-tuple-element.28.ll_ref), custom_call_target="tpu_custom_call" | custom-call | tf_op jit(solution)/shard_map/pallas_call | solution.py:275
  29.2 0.3 collective-permute-done.5.refs_4_
  29.5 1.2 %collective-permute-done.7.refs_6_ = f32[16,1536]{1,0:T(8,128)S(1)} collective-permute-done((f32[16,1536]{1,0:T(8,128)S(1)}, f32[16,1536]{1,0:T(8,128)S(1)}, u32[]{:S(2)}, u32[]{:S(2)}) %collective-permute-start.7) | collective-permute-done | bytes 98336 | tf_op jit(solution)/shard_map/ppermute | solution.py:239
  30.7 1.2 %shard_map.46 = (f32[16,3072]{1,0:T(8,128)S(1)}, f32[16,1536]{1,0:T(8,128)S(1)}, f32[16,1536]{1,0:T(8,128)S(1)}, f32[16,1536]{1,0:T(8,128)S(1)}, f32[16,1536]{1,0:T(8,128)S(1)}) custom-call(f32[16,3072]{1,0:T(8,128)S(1)} %shard_map.45.refs_0_, f32[16,3072]{1,0:T(8,128)S(1)} %get-tuple-element.35.p_ref.refs_1_.refs_2_.b1, ...), custom_call_target="tpu_custom_call" | custom-call | tf_op jit(solution)/shard_map/pallas_call | solution.py:278
  31.9 0.0 collective-permute-start.8
  32.0 2.9 %collective-permute-start.9 = (f32[16,1536]{1,0:T(8,128)S(1)}, f32[16,1536]{1,0:T(8,128)S(1)}, u32[]{:S(2)}, u32[]{:S(2)}) collective-permute-start(f32[16,1536]{1,0:T(8,128)S(1)} %get-tuple-element.42), channel_id=1, source_target_pairs={{8,16},{24,32},{40,48},{56,64},{72,80},{88,96},{104,112},{120,128}... | collective-permute-start | bytes 294920 | tf_op jit(solution)/shard_map/ppermute | solution.py:241
  34.8 1.5 %collective-permute-start.10 = (f32[16,1536]{1,0:T(8,128)S(1)}, f32[16,1536]{1,0:T(8,128)S(1)}, u32[]{:S(2)}, u32[]{:S(2)}) collective-permute-start(f32[16,1536]{1,0:T(8,128)S(1)} %get-tuple-element.43), channel_id=1, source_target_pairs={{0,1},{1,0},{2,3},{3,2},{4,5},{5,4},{6,7},{7,6},{8,9},{9,8},{10,11... | collective-permute-start | bytes 294920 | tf_op jit(solution)/shard_map/ppermute | solution.py:240
  36.3 1.0 %collective-permute-start.11 = (f32[16,1536]{1,0:T(8,128)S(1)}, f32[16,1536]{1,0:T(8,128)S(1)}, u32[]{:S(2)}, u32[]{:S(2)}) collective-permute-start(f32[16,1536]{1,0:T(8,128)S(1)} %get-tuple-element.44), channel_id=1, source_target_pairs={{1,2},{3,4},{5,6},{7,0},{2,1},{4,3},{6,5},{0,7},{9,10},{11,12},{13... | collective-permute-start | bytes 294920 | tf_op jit(solution)/shard_map/ppermute | solution.py:239
  37.3 2.0 %shard_map.47.refs_0_ = f32[16,3072]{1,0:T(8,128)S(1)} custom-call(f32[16,3072]{1,0:T(8,128)S(1)} %get-tuple-element.40.p_ref.refs_1_.refs_2_.b2, bf16[2,12,128,384]{3,2,1,0:T(8,128)(2,1)S(1)} %get-tuple-element.27.lh_ref, bf16[2,12,128,384]{3,2,1,0:T(8,128)(2,1)S(1)} %get-tuple-element.28.ll_ref), custom_call_target="tpu_custom_call" | custom-call | tf_op jit(solution)/shard_map/pallas_call | solution.py:275
  39.4 0.0 collective-permute-done.10.refs_5_
  39.5 1.5 %collective-permute-done.11.refs_6_ = f32[16,1536]{1,0:T(8,128)S(1)} collective-permute-done((f32[16,1536]{1,0:T(8,128)S(1)}, f32[16,1536]{1,0:T(8,128)S(1)}, u32[]{:S(2)}, u32[]{:S(2)}) %collective-permute-start.11) | collective-permute-done | bytes 98336 | tf_op jit(solution)/shard_map/ppermute | solution.py:239
  40.9 1.2 %shard_map.48 = (f32[16,3072]{1,0:T(8,128)S(1)}, f32[16,1536]{1,0:T(8,128)S(1)}, f32[16,1536]{1,0:T(8,128)S(1)}, f32[16,1536]{1,0:T(8,128)S(1)}, f32[16,1536]{1,0:T(8,128)S(1)}) custom-call(f32[16,3072]{1,0:T(8,128)S(1)} %shard_map.47.refs_0_, f32[16,3072]{1,0:T(8,128)S(1)} %get-tuple-element.40.p_ref.refs_1_.refs_2_.b2, ...), custom_call_target="tpu_custom_call" | custom-call | tf_op jit(solution)/shard_map/pallas_call | solution.py:278
  42.2 1.3 %collective-permute-start.13 = (f32[16,1536]{1,0:T(8,128)S(1)}, f32[16,1536]{1,0:T(8,128)S(1)}, u32[]{:S(2)}, u32[]{:S(2)}) collective-permute-start(f32[16,1536]{1,0:T(8,128)S(1)} %get-tuple-element.47), channel_id=1, source_target_pairs={{8,16},{24,32},{40,48},{56,64},{72,80},{88,96},{104,112},{120,128}... | collective-permute-start | bytes 294920 | tf_op jit(solution)/shard_map/ppermute | solution.py:241
  43.5 1.5 %collective-permute-start.14 = (f32[16,1536]{1,0:T(8,128)S(1)}, f32[16,1536]{1,0:T(8,128)S(1)}, u32[]{:S(2)}, u32[]{:S(2)}) collective-permute-start(f32[16,1536]{1,0:T(8,128)S(1)} %get-tuple-element.48), channel_id=1, source_target_pairs={{0,1},{1,0},{2,3},{3,2},{4,5},{5,4},{6,7},{7,6},{8,9},{9,8},{10,11... | collective-permute-start | bytes 294920 | tf_op jit(solution)/shard_map/ppermute | solution.py:240
  45.0 1.0 collective-permute-start.15
  46.0 2.0 %shard_map.49.refs_0_ = f32[16,3072]{1,0:T(8,128)S(1)} custom-call(f32[16,3072]{1,0:T(8,128)S(1)} %get-tuple-element.45.p_ref.refs_1_.refs_3_.b3, bf16[2,12,128,384]{3,2,1,0:T(8,128)(2,1)S(1)} %get-tuple-element.27.lh_ref, bf16[2,12,128,384]{3,2,1,0:T(8,128)(2,1)S(1)} %get-tuple-element.28.ll_ref), custom_call_target="tpu_custom_call" | custom-call | tf_op jit(solution)/shard_map/pallas_call | solution.py:275
  48.1 1.5 %collective-permute-done.13.refs_4_ = f32[16,1536]{1,0:T(8,128)S(1)} collective-permute-done((f32[16,1536]{1,0:T(8,128)S(1)}, f32[16,1536]{1,0:T(8,128)S(1)}, u32[]{:S(2)}, u32[]{:S(2)}) %collective-permute-start.13) | collective-permute-done | bytes 98336 | tf_op jit(solution)/shard_map/ppermute | solution.py:241
  49.6 1.1 %shard_map.50.refs_4_.b4 = f32[16,3072]{1,0:T(8,128)S(1)} custom-call(f32[16,3072]{1,0:T(8,128)S(1)} %shard_map.49.refs_0_, f32[16,3072]{1,0:T(8,128)S(1)} %get-tuple-element.45.p_ref.refs_1_.refs_3_.b3, f32[16,3072]{1,0:T(8,128)S(1)} %get-tuple-element.40.p_ref.refs_1_.refs_2_.b2, f32[16,1536]{1,0:T(8,128)S(1)} %collective-permute-done.12.refs_3_, ...), custom_call_target="tpu_custom_call" | custom-call | tf_op jit(solution)/shard_map/pallas_call | solution.py:278
  50.7 1.0 shard_map.51
  51.7 0.1 collective-permute-start.16
  51.8 1.2 %collective-permute-done.16 = f32[80,128]{1,0:T(8,128)S(1)} collective-permute-done((f32[80,128]{1,0:T(8,128)S(1)}, f32[80,128]{1,0:T(8,128)S(1)}, u32[]{:S(2)}, u32[]{:S(2)}) %collective-permute-start.16) | collective-permute-done | bytes 40992 | tf_op jit(solution)/shard_map/ppermute | solution.py:250
  53.0 1.0 %collective-permute-start.17 = (f32[80,128]{1,0:T(8,128)S(1)}, f32[80,128]{1,0:T(8,128)S(1)}, u32[]{:S(2)}, u32[]{:S(2)}) collective-permute-start(f32[80,128]{1,0:T(8,128)S(1)} %add.24), channel_id=1, source_target_pairs={{0,16},{8,24},{16,0},{24,8},{32,48},{40,56},{48,32},{56,40},{64,80... | collective-permute-start | bytes 122888 | tf_op jit(solution)/shard_map/ppermute | solution.py:250
  54.0 3.0 %collective-permute-done.17 = f32[80,128]{1,0:T(8,128)S(1)} collective-permute-done((f32[80,128]{1,0:T(8,128)S(1)}, f32[80,128]{1,0:T(8,128)S(1)}, u32[]{:S(2)}, u32[]{:S(2)}) %collective-permute-start.17) | collective-permute-done | bytes 40992 | tf_op jit(solution)/shard_map/ppermute | solution.py:250
  57.0 0.1 collective-permute-start.18
  57.1 5.2 %collective-permute-done.18 = f32[80,128]{1,0:T(8,128)S(1)} collective-permute-done((f32[80,128]{1,0:T(8,128)S(1)}, f32[80,128]{1,0:T(8,128)S(1)}, u32[]{:S(2)}, u32[]{:S(2)}) %collective-permute-start.18) | collective-permute-done | bytes 40992 | tf_op jit(solution)/shard_map/ppermute | solution.py:250
  62.3 4.0 %collective-permute-done.19 = f32[80,128]{1,0:T(8,128)S(1)} collective-permute-done((f32[80,128]{1,0:T(8,128)S(1)}, f32[80,128]{1,0:T(8,128)S(1)}, u32[]{:S(2)}, u32[]{:S(2)}) %collective-permute-start.19) | collective-permute-done | bytes 40992 | tf_op jit(solution)/shard_map/ppermute | solution.py:250
  66.3 5.2 %collective-permute-done.20 = f32[80,128]{1,0:T(8,128)S(1)} collective-permute-done((f32[80,128]{1,0:T(8,128)S(1)}, f32[80,128]{1,0:T(8,128)S(1)}, u32[]{:S(2)}, u32[]{:S(2)}) %collective-permute-start.20) | collective-permute-done | bytes 40992 | tf_op jit(solution)/shard_map/ppermute | solution.py:250
  71.5 1.7 %collective-permute-start.21 = (f32[80,128]{1,0:T(8,128)S(1)}, f32[80,128]{1,0:T(8,128)S(1)}, u32[]{:S(2)}, u32[]{:S(2)}) collective-permute-start(f32[80,128]{1,0:T(8,128)S(1)} %add.28), channel_id=1, source_target_pairs={{0,1},{1,0},{2,3},{3,2},{4,5},{5,4},{6,7},{7,6},{8,9},{9,8},{10,11... | collective-permute-start | bytes 122888 | tf_op jit(solution)/shard_map/ppermute | solution.py:250
  73.2 2.3 %collective-permute-done.21 = f32[80,128]{1,0:T(8,128)S(1)} collective-permute-done((f32[80,128]{1,0:T(8,128)S(1)}, f32[80,128]{1,0:T(8,128)S(1)}, u32[]{:S(2)}, u32[]{:S(2)}) %collective-permute-start.21) | collective-permute-done | bytes 40992 | tf_op jit(solution)/shard_map/ppermute | solution.py:250
  75.5 2.2 %collective-permute-start.22 = (f32[80,128]{1,0:T(8,128)S(1)}, f32[80,128]{1,0:T(8,128)S(1)}, u32[]{:S(2)}, u32[]{:S(2)}) collective-permute-start(f32[80,128]{1,0:T(8,128)S(1)} %add.29), channel_id=1, source_target_pairs={{0,2},{1,3},{2,0},{3,1},{4,6},{5,7},{6,4},{7,5},{8,10},{9,11},{10,... | collective-permute-start | bytes 122888 | tf_op jit(solution)/shard_map/ppermute | solution.py:250
  77.7 3.0 %collective-permute-done.22 = f32[80,128]{1,0:T(8,128)S(1)} collective-permute-done((f32[80,128]{1,0:T(8,128)S(1)}, f32[80,128]{1,0:T(8,128)S(1)}, u32[]{:S(2)}, u32[]{:S(2)}) %collective-permute-start.22) | collective-permute-done | bytes 40992 | tf_op jit(solution)/shard_map/ppermute | solution.py:250
  80.6 2.7 %collective-permute-start.23 = (f32[80,128]{1,0:T(8,128)S(1)}, f32[80,128]{1,0:T(8,128)S(1)}, u32[]{:S(2)}, u32[]{:S(2)}) collective-permute-start(f32[80,128]{1,0:T(8,128)S(1)} %add.30), channel_id=1, source_target_pairs={{0,7},{1,6},{2,5},{3,4},{4,3},{5,2},{6,1},{7,0},{8,15},{9,14},{10,... | collective-permute-start | bytes 122888 | tf_op jit(solution)/shard_map/ppermute | solution.py:250
  83.4 4.3 %collective-permute-done.23 = f32[80,128]{1,0:T(8,128)S(1)} collective-permute-done((f32[80,128]{1,0:T(8,128)S(1)}, f32[80,128]{1,0:T(8,128)S(1)}, u32[]{:S(2)}, u32[]{:S(2)}) %collective-permute-start.23) | collective-permute-done | bytes 40992 | tf_op jit(solution)/shard_map/ppermute | solution.py:250
  87.7 12.8 %shard_map.52 = (f32[2,2,12,64,80]{4,3,2,1,0:T(8,128)}, f32[80,80]{1,0:T(8,128)}) custom-call(f32[80,128]{1,0:T(8,128)S(1)} %add.31.g_ref, f32[16,3072]{1,0:T(8,128)S(1)} %get-tuple-element.26.p_ref.refs_1_.refs_2_.refs_0_.b0, f32[16,3072]{1,0:T(8,128)S(1)} %get-tuple-element.35.p_ref.refs_1_.refs_2_.b1, ...), custom_call_target="tpu_custom_call" | custom-call | tf_op jit(solution)/shard_map/pallas_call | solution.py:290
  (24 shorter events, 0.1 us)
Async XLA Ops:
  0.6 1.0 copy-start.1
  1.8 18.9 %collective-permute-start = (f32[16,1536]{1,0:T(8,128)S(1)}, f32[16,1536]{1,0:T(8,128)S(1)}, u32[]{:S(2)}, u32[]{:S(2)}) collective-permute-start(f32[16,1536]{1,0:T(8,128)S(1)} %get-tuple-element.29), channel_id=1, source_target_pairs={{0,8},{8,0},{16,24},{24,16},{32,40},{40,32},{48,56},{56,48},{64,72... | collective-permute-start | bytes 294920 | tf_op jit(solution)/shard_map/ppermute | solution.py:242
  1.9 18.8 %collective-permute-start.1 = (f32[16,1536]{1,0:T(8,128)S(1)}, f32[16,1536]{1,0:T(8,128)S(1)}, u32[]{:S(2)}, u32[]{:S(2)}) collective-permute-start(f32[16,1536]{1,0:T(8,128)S(1)} %get-tuple-element.30), channel_id=1, source_target_pairs={{8,16},{24,32},{40,48},{56,64},{72,80},{88,96},{104,112},{120,128}... | collective-permute-start | bytes 294920 | tf_op jit(solution)/shard_map/ppermute | solution.py:241
  7.3 13.5 %collective-permute-start.2 = (f32[16,1536]{1,0:T(8,128)S(1)}, f32[16,1536]{1,0:T(8,128)S(1)}, u32[]{:S(2)}, u32[]{:S(2)}) collective-permute-start(f32[16,1536]{1,0:T(8,128)S(1)} %get-tuple-element.31), channel_id=1, source_target_pairs={{0,1},{1,0},{2,3},{3,2},{4,5},{5,4},{6,7},{7,6},{8,9},{9,8},{10,11... | collective-permute-start | bytes 294920 | tf_op jit(solution)/shard_map/ppermute | solution.py:240
  7.4 13.4 %collective-permute-start.3 = (f32[16,1536]{1,0:T(8,128)S(1)}, f32[16,1536]{1,0:T(8,128)S(1)}, u32[]{:S(2)}, u32[]{:S(2)}) collective-permute-start(f32[16,1536]{1,0:T(8,128)S(1)} %get-tuple-element.32), channel_id=1, source_target_pairs={{1,2},{3,4},{5,6},{7,0},{2,1},{4,3},{6,5},{0,7},{9,10},{11,12},{13... | collective-permute-start | bytes 294920 | tf_op jit(solution)/shard_map/ppermute | solution.py:239
  11.1 4.1 %copy-start = (f32[2,2,12,7,64,64]{5,4,3,2,1,0:T(8,128)S(1)}, f32[2,2,12,7,64,64]{5,4,3,2,1,0:T(8,128)}, u32[]{:S(2)}) copy-start(f32[2,2,12,7,64,64]{5,4,3,2,1,0:T(8,128)} %a_ref.1) | copy-start | bytes 16515076
  22.0 7.2 %collective-permute-start.4 = (f32[16,1536]{1,0:T(8,128)S(1)}, f32[16,1536]{1,0:T(8,128)S(1)}, u32[]{:S(2)}, u32[]{:S(2)}) collective-permute-start(f32[16,1536]{1,0:T(8,128)S(1)} %get-tuple-element.36), channel_id=1, source_target_pairs={{0,8},{8,0},{16,24},{24,16},{32,40},{40,32},{48,56},{56,48},{64,72... | collective-permute-start | bytes 294920 | tf_op jit(solution)/shard_map/ppermute | solution.py:242
  22.0 7.4 %collective-permute-start.5 = (f32[16,1536]{1,0:T(8,128)S(1)}, f32[16,1536]{1,0:T(8,128)S(1)}, u32[]{:S(2)}, u32[]{:S(2)}) collective-permute-start(f32[16,1536]{1,0:T(8,128)S(1)} %get-tuple-element.37), channel_id=1, source_target_pairs={{8,16},{24,32},{40,48},{56,64},{72,80},{88,96},{104,112},{120,128}... | collective-permute-start | bytes 294920 | tf_op jit(solution)/shard_map/ppermute | solution.py:241
  23.0 6.5 %collective-permute-start.6 = (f32[16,1536]{1,0:T(8,128)S(1)}, f32[16,1536]{1,0:T(8,128)S(1)}, u32[]{:S(2)}, u32[]{:S(2)}) collective-permute-start(f32[16,1536]{1,0:T(8,128)S(1)} %get-tuple-element.38), channel_id=1, source_target_pairs={{0,1},{1,0},{2,3},{3,2},{4,5},{5,4},{6,7},{7,6},{8,9},{9,8},{10,11... | collective-permute-start | bytes 294920 | tf_op jit(solution)/shard_map/ppermute | solution.py:240
  26.1 4.6 %collective-permute-start.7 = (f32[16,1536]{1,0:T(8,128)S(1)}, f32[16,1536]{1,0:T(8,128)S(1)}, u32[]{:S(2)}, u32[]{:S(2)}) collective-permute-start(f32[16,1536]{1,0:T(8,128)S(1)} %get-tuple-element.39), channel_id=1, source_target_pairs={{1,2},{3,4},{5,6},{7,0},{2,1},{4,3},{6,5},{0,7},{9,10},{11,12},{13... | collective-permute-start | bytes 294920 | tf_op jit(solution)/shard_map/ppermute | solution.py:239
  31.9 7.5 %collective-permute-start.8 = (f32[16,1536]{1,0:T(8,128)S(1)}, f32[16,1536]{1,0:T(8,128)S(1)}, u32[]{:S(2)}, u32[]{:S(2)}) collective-permute-start(f32[16,1536]{1,0:T(8,128)S(1)} %get-tuple-element.41), channel_id=1, source_target_pairs={{0,8},{8,0},{16,24},{24,16},{32,40},{40,32},{48,56},{56,48},{64,72... | collective-permute-start | bytes 294920 | tf_op jit(solution)/shard_map/ppermute | solution.py:242
  32.0 7.4 %collective-permute-start.9 = (f32[16,1536]{1,0:T(8,128)S(1)}, f32[16,1536]{1,0:T(8,128)S(1)}, u32[]{:S(2)}, u32[]{:S(2)}) collective-permute-start(f32[16,1536]{1,0:T(8,128)S(1)} %get-tuple-element.42), channel_id=1, source_target_pairs={{8,16},{24,32},{40,48},{56,64},{72,80},{88,96},{104,112},{120,128}... | collective-permute-start | bytes 294920 | tf_op jit(solution)/shard_map/ppermute | solution.py:241
  34.8 4.6 %collective-permute-start.10 = (f32[16,1536]{1,0:T(8,128)S(1)}, f32[16,1536]{1,0:T(8,128)S(1)}, u32[]{:S(2)}, u32[]{:S(2)}) collective-permute-start(f32[16,1536]{1,0:T(8,128)S(1)} %get-tuple-element.43), channel_id=1, source_target_pairs={{0,1},{1,0},{2,3},{3,2},{4,5},{5,4},{6,7},{7,6},{8,9},{9,8},{10,11... | collective-permute-start | bytes 294920 | tf_op jit(solution)/shard_map/ppermute | solution.py:240
  36.3 4.6 %collective-permute-start.11 = (f32[16,1536]{1,0:T(8,128)S(1)}, f32[16,1536]{1,0:T(8,128)S(1)}, u32[]{:S(2)}, u32[]{:S(2)}) collective-permute-start(f32[16,1536]{1,0:T(8,128)S(1)} %get-tuple-element.44), channel_id=1, source_target_pairs={{1,2},{3,4},{5,6},{7,0},{2,1},{4,3},{6,5},{0,7},{9,10},{11,12},{13... | collective-permute-start | bytes 294920 | tf_op jit(solution)/shard_map/ppermute | solution.py:239
  42.1 5.9 %collective-permute-start.12 = (f32[16,1536]{1,0:T(8,128)S(1)}, f32[16,1536]{1,0:T(8,128)S(1)}, u32[]{:S(2)}, u32[]{:S(2)}) collective-permute-start(f32[16,1536]{1,0:T(8,128)S(1)} %get-tuple-element.46), channel_id=1, source_target_pairs={{0,8},{8,0},{16,24},{24,16},{32,40},{40,32},{48,56},{56,48},{64,72... | collective-permute-start | bytes 294920 | tf_op jit(solution)/shard_map/ppermute | solution.py:242
  42.2 7.4 %collective-permute-start.13 = (f32[16,1536]{1,0:T(8,128)S(1)}, f32[16,1536]{1,0:T(8,128)S(1)}, u32[]{:S(2)}, u32[]{:S(2)}) collective-permute-start(f32[16,1536]{1,0:T(8,128)S(1)} %get-tuple-element.47), channel_id=1, source_target_pairs={{8,16},{24,32},{40,48},{56,64},{72,80},{88,96},{104,112},{120,128}... | collective-permute-start | bytes 294920 | tf_op jit(solution)/shard_map/ppermute | solution.py:241
  43.5 6.1 %collective-permute-start.14 = (f32[16,1536]{1,0:T(8,128)S(1)}, f32[16,1536]{1,0:T(8,128)S(1)}, u32[]{:S(2)}, u32[]{:S(2)}) collective-permute-start(f32[16,1536]{1,0:T(8,128)S(1)} %get-tuple-element.48), channel_id=1, source_target_pairs={{0,1},{1,0},{2,3},{3,2},{4,5},{5,4},{6,7},{7,6},{8,9},{9,8},{10,11... | collective-permute-start | bytes 294920 | tf_op jit(solution)/shard_map/ppermute | solution.py:240
  45.0 4.6 %collective-permute-start.15 = (f32[16,1536]{1,0:T(8,128)S(1)}, f32[16,1536]{1,0:T(8,128)S(1)}, u32[]{:S(2)}, u32[]{:S(2)}) collective-permute-start(f32[16,1536]{1,0:T(8,128)S(1)} %get-tuple-element.49), channel_id=1, source_target_pairs={{1,2},{3,4},{5,6},{7,0},{2,1},{4,3},{6,5},{0,7},{9,10},{11,12},{13... | collective-permute-start | bytes 294920 | tf_op jit(solution)/shard_map/ppermute | solution.py:239
  51.7 1.3 %collective-permute-start.16 = (f32[80,128]{1,0:T(8,128)S(1)}, f32[80,128]{1,0:T(8,128)S(1)}, u32[]{:S(2)}, u32[]{:S(2)}) collective-permute-start(f32[80,128]{1,0:T(8,128)S(1)} %shard_map.51), channel_id=1, source_target_pairs={{0,8},{8,0},{16,24},{24,16},{32,40},{40,32},{48,56},{56,48},{64,72... | collective-permute-start | bytes 122888 | tf_op jit(solution)/shard_map/ppermute | solution.py:250
  53.0 4.0 %collective-permute-start.17 = (f32[80,128]{1,0:T(8,128)S(1)}, f32[80,128]{1,0:T(8,128)S(1)}, u32[]{:S(2)}, u32[]{:S(2)}) collective-permute-start(f32[80,128]{1,0:T(8,128)S(1)} %add.24), channel_id=1, source_target_pairs={{0,16},{8,24},{16,0},{24,8},{32,48},{40,56},{48,32},{56,40},{64,80... | collective-permute-start | bytes 122888 | tf_op jit(solution)/shard_map/ppermute | solution.py:250
  57.0 5.2 %collective-permute-start.18 = (f32[80,128]{1,0:T(8,128)S(1)}, f32[80,128]{1,0:T(8,128)S(1)}, u32[]{:S(2)}, u32[]{:S(2)}) collective-permute-start(f32[80,128]{1,0:T(8,128)S(1)} %add.25), channel_id=1, source_target_pairs={{0,48},{8,56},{16,32},{24,40},{32,16},{40,24},{48,0},{56,8},{64,11... | collective-permute-start | bytes 122888 | tf_op jit(solution)/shard_map/ppermute | solution.py:250
  62.2 4.0 %collective-permute-start.19 = (f32[80,128]{1,0:T(8,128)S(1)}, f32[80,128]{1,0:T(8,128)S(1)}, u32[]{:S(2)}, u32[]{:S(2)}) collective-permute-start(f32[80,128]{1,0:T(8,128)S(1)} %add.26), channel_id=1, source_target_pairs={{0,64},{8,72},{16,80},{24,88},{32,96},{40,104},{48,112},{56,120},{... | collective-permute-start | bytes 122888 | tf_op jit(solution)/shard_map/ppermute | solution.py:250
  66.3 5.2 %collective-permute-start.20 = (f32[80,128]{1,0:T(8,128)S(1)}, f32[80,128]{1,0:T(8,128)S(1)}, u32[]{:S(2)}, u32[]{:S(2)}) collective-permute-start(f32[80,128]{1,0:T(8,128)S(1)} %add.27), channel_id=1, source_target_pairs={{0,192},{8,200},{16,208},{24,216},{32,224},{40,232},{48,240},{56,2... | collective-permute-start | bytes 122888 | tf_op jit(solution)/shard_map/ppermute | solution.py:250
  71.5 4.0 %collective-permute-start.21 = (f32[80,128]{1,0:T(8,128)S(1)}, f32[80,128]{1,0:T(8,128)S(1)}, u32[]{:S(2)}, u32[]{:S(2)}) collective-permute-start(f32[80,128]{1,0:T(8,128)S(1)} %add.28), channel_id=1, source_target_pairs={{0,1},{1,0},{2,3},{3,2},{4,5},{5,4},{6,7},{7,6},{8,9},{9,8},{10,11... | collective-permute-start | bytes 122888 | tf_op jit(solution)/shard_map/ppermute | solution.py:250
  75.5 5.1 %collective-permute-start.22 = (f32[80,128]{1,0:T(8,128)S(1)}, f32[80,128]{1,0:T(8,128)S(1)}, u32[]{:S(2)}, u32[]{:S(2)}) collective-permute-start(f32[80,128]{1,0:T(8,128)S(1)} %add.29), channel_id=1, source_target_pairs={{0,2},{1,3},{2,0},{3,1},{4,6},{5,7},{6,4},{7,5},{8,10},{9,11},{10,... | collective-permute-start | bytes 122888 | tf_op jit(solution)/shard_map/ppermute | solution.py:250
  80.6 7.0 %collective-permute-start.23 = (f32[80,128]{1,0:T(8,128)S(1)}, f32[80,128]{1,0:T(8,128)S(1)}, u32[]{:S(2)}, u32[]{:S(2)}) collective-permute-start(f32[80,128]{1,0:T(8,128)S(1)} %add.30), channel_id=1, source_target_pairs={{0,7},{1,6},{2,5},{3,4},{4,3},{5,2},{6,1},{7,0},{8,15},{9,14},{10,... | collective-permute-start | bytes 122888 | tf_op jit(solution)/shard_map/ppermute | solution.py:250
where the time goes:
time: 101 us; the launch traced here: 100 us
  waiting for transfers between devices  32.7 us (32%)
  starting transfers between devices  31.5 us (31%)
  Pallas kernels  30.3 us (30%)
  local copies, waits for them, and re-layouts  5.12 us (5%)
    ppermute x8, waiting for transfers between devices, total_over_devices(): lax.ppermute(gram, axis, [(i, i ^ mask) for i in range(count)])  28 us
    pallas_call x1, Pallas kernels, per_device(): call(finish_kernel, [((2, 2, Z, U, COLS), F32), ((COLS, COLS), F32)], 1 +...  12.8 us
    ppermute x4, starting transfers between devices, exchange(): o = lax.ppermute(o, 'gx', odd(wide))  10.5 us
    pallas_call x4, Pallas kernels, per_device(): part = call(local_kernel, BLOCK, 3)(blocks[-1], local_high, local_low)  8.2 us
    ppermute x8, starting transfers between devices, total_over_devices(): lax.ppermute(gram, axis, [(i, i ^ mask) for i in range(count)])  7.83 us
    ppermute x4, starting transfers between devices, exchange(): oo = lax.ppermute(oo, 'gy', odd(deep))  6.75 us
    ppermute x4, starting transfers between devices, exchange(): ee = lax.ppermute(ee, 'gy', even(deep))  6.23 us
    unnamed x4, local copies, waits for them, and re-layouts  5.12 us
  transfers between devices with their start and end apart: 24, of which 12 were waited for; matrix products, arithmetic and copies ran while one was open for 0% of the time, Pallas kernels for 12%

commit v1 on v0

v1 whole, which is shorter than its diff:
```python
import functools

import jax
import jax.numpy as jnp
from jax import lax
from jax.experimental import pallas as pl
from jax.experimental.pallas import tpu as pltpu
from jax.sharding import PartitionSpec as P

F32 = jnp.float32
BF16 = jnp.bfloat16
Z = 12
R = 16
U = 64
L = 2 * U
FACE = Z * L
WIDE = 2 * FACE
STEPS = 4
COLS = (STEPS + 1) * R
VMEM_LIMIT = 16 * 1024 * 1024
NT = (((1,), (1,)), ((), ()))
TN = (((0,), (0,)), ((), ()))

VM = pl.BlockSpec(memory_space=pltpu.VMEM)


def low_lanes(shape):
    return lax.broadcasted_iota(jnp.int32, shape, len(shape) - 1) < U


def split(value):
    high = value.astype(BF16)
    return high, (value - high.astype(F32)).astype(BF16)


def product(left, w_high, w_low):
    high, low = split(left)
    both = lax.dot_general(
        jnp.concatenate([high, low], axis=0), w_high, NT, preferred_element_type=F32
    )
    rest = lax.dot_general(high, w_low, NT, preferred_element_type=F32)
    total = both[: 2 * R] + both[2 * R :] + rest
    return jnp.where(low_lanes((R, L)), total[:R], total[R:])


def swapped(pair):
    return pltpu.roll(pair, U, 1)


def parity():
    return lax.axis_index("gx") & 1, lax.axis_index("gy") & 1


def lanes(x, z):
    base = (x * Z + z) * L
    return slice(base, base + L)


def store_packets(pairs, px, py, e_ref, o_ref, ee_ref, oo_ref):
    low = low_lanes((R, L))
    for z in range(Z):
        at = slice(z * L, (z + 1) * L)
        first, second = pairs[0][z], pairs[1][z]
        e_ref[:, at] = jnp.where(px == 0, second, first)
        o_ref[:, at] = jnp.where(px == 0, first, second)
        face0 = jnp.where(low, first, swapped(second))
        face1 = jnp.where(low, swapped(first), second)
        ee_ref[:, at] = jnp.where(py == 0, face1, face0)
        oo_ref[:, at] = jnp.where(py == 0, face0, face1)


def begin_kernel(s_ref, p_ref, e_ref, o_ref, ee_ref, oo_ref):
    px, py = parity()
    pairs = [[None] * Z for _ in range(2)]
    for x in range(2):
        for z in range(Z):
            pair = jnp.concatenate([s_ref[x, 0, z], s_ref[x, 1, z]], axis=1)
            p_ref[:, lanes(x, z)] = pair
            pairs[x][z] = pair
    store_packets(pairs, px, py, e_ref, o_ref, ee_ref, oo_ref)


def neighbour_rows(p_ref):
    low = low_lanes((R, L))
    pairs = [[p_ref[:, lanes(x, z)] for z in range(Z)] for x in range(2)]
    turned = [[swapped(v) for v in row] for row in pairs]
    zero = jnp.zeros((R, L), F32)

    def at(rows, x, z):
        return rows[x][z] if 0 <= z < Z else zero

    def left(x, z):
        a = [
            jnp.where(low, pairs[x][z], turned[1 - x][z]),
            jnp.where(low, at(pairs, x, z - 1), at(turned, x, z + 1)),
            turned[x][z],
        ]
        b = [
            jnp.where(low, turned[x][z], pairs[1 - x][z]),
            jnp.where(low, at(turned, x, z - 1), at(pairs, x, z + 1)),
            pairs[x][z],
        ]
        return jnp.concatenate([jnp.concatenate(a, axis=1), jnp.concatenate(b, axis=1)], axis=0)

    return left


def gram_row(blocks):
    tall = jnp.concatenate(blocks, axis=0)
    row = lax.dot_general(
        blocks[-1], tall, NT, precision=lax.Precision.HIGHEST, preferred_element_type=F32
    )
    return jnp.concatenate([row, jnp.zeros((R, L - row.shape[1]), F32)], axis=1)


def first_kernel(a_ref, p_ref, lh_ref, ll_ref, eh_ref, el_ref, out_ref, g_ref, buffer, arrived):
    copies = [
        pltpu.make_async_copy(a_ref.at[:, :, z], buffer.at[z], arrived.at[z]) for z in range(Z)
    ]
    for copy in copies:
        copy.start()
    g_ref[...] = gram_row([p_ref[...]])
    left = neighbour_rows(p_ref)
    zero = jnp.zeros((U, U), F32)
    for z in range(Z):
        copies[z].wait()
        for x in range(2):
            for y in range(2):
                rows = slice(y * U, (y + 1) * U)
                f = [buffer[z, x, y, k] for k in range(7)]
                tiles = ((f[0], f[2 - x]), (f[5], f[6]), (f[4 - y], zero))
                for t, both in enumerate(tiles):
                    high, low = split(jnp.concatenate(both, axis=1))
                    lh_ref[x, z, rows, t * L : (t + 1) * L] = high
                    ll_ref[x, z, rows, t * L : (t + 1) * L] = low
                along_x, along_y = f[1 + x], f[3 + y]
                outer = (along_y, along_x) if x == 0 else (along_x, along_y)
                eh_ref[x, z, rows, :], el_ref[x, z, rows, :] = split(jnp.concatenate(outer, axis=1))
            out_ref[:, lanes(x, z)] = product(left(x, z), lh_ref[x, z], ll_ref[x, z])


def local_kernel(lh_ref, ll_ref, *refs):
    *blocks, out_ref, g_ref = refs
    left = neighbour_rows(blocks[-1])
    for x in range(2):
        for z in range(Z):
            out_ref[:, lanes(x, z)] = product(left(x, z), lh_ref[x, z], ll_ref[x, z])
    g_ref[...] = gram_row([b[...] for b in blocks])


def outer_kernel(step, *refs):
    first, last = step == 0, step == STEPS - 1
    blocks, refs = refs[: step + 1], refs[step + 1 :]
    if last:
        rows, refs = refs[:STEPS], refs[STEPS:]
    part_ref, e_ref, o_ref, ee_ref, oo_ref, eh_ref, el_ref, new_ref, *outs = refs
    px, py = parity()
    low = low_lanes((R, L))
    gx, gy = lax.axis_index("gx"), lax.axis_index("gy")
    o_there = jnp.logical_and(gx > 0, gx < lax.axis_size("gx") - 1)
    oo_there = jnp.logical_and(gy > 0, gy < lax.axis_size("gy") - 1)
    pairs = [[None] * Z for _ in range(2)]
    for z in range(Z):
        at = slice(z * L, (z + 1) * L)
        e, o, ee, oo = e_ref[:, at], o_ref[:, at], ee_ref[:, at], oo_ref[:, at]
        o = jnp.where(o_there, o, 0.0)
        oo = jnp.where(oo_there, oo, 0.0)
        x0, x1 = jnp.where(px == 0, o, e), jnp.where(px == 0, e, o)
        ym, yp = jnp.where(py == 0, oo, ee), jnp.where(py == 0, ee, oo)
        left0 = jnp.concatenate([jnp.where(low, ym, swapped(x0)), jnp.where(low, yp, x0)], axis=0)
        left1 = jnp.concatenate([jnp.where(low, x1, ym), jnp.where(low, swapped(x1), yp)], axis=0)
        for x, left in ((0, left0), (1, left1)):
            here = lanes(x, z)
            applied = part_ref[:, here] + product(left, eh_ref[x, z], el_ref[x, z])
            shifted = (applied - 8.0 * blocks[-1][:, here]) * (1.0 / 6.0)
            pairs[x][z] = shifted if first else 2.0 * shifted - blocks[-2][:, here]
            new_ref[:, here] = pairs[x][z]
    if not last:
        store_packets(pairs, px, py, *outs)
        return
    newest = jnp.concatenate(pairs[0] + pairs[1], axis=1)
    row4 = gram_row([b[...] for b in blocks] + [newest])
    row0, row1, row2, row3 = (r[...] for r in rows)
    outs[0][:R, :] = row4 + pltpu.roll(row2, 5 * R, 1)
    outs[0][R:, :] = row3 + pltpu.roll(row1, 4 * R, 1) + pltpu.roll(row0, 6 * R, 1)


def unpacked(g_ref):
    one, two = g_ref[:R, :], g_ref[R:, :]
    shifted = [
        pltpu.roll(two, L - 6 * R, 1),
        pltpu.roll(two, L - 4 * R, 1),
        pltpu.roll(one, L - 5 * R, 1),
        two,
        one,
    ]
    lane = lax.broadcasted_iota(jnp.int32, (R, L), 1)
    rows = [jnp.where(lane < (k + 1) * R, row, 0.0) for k, row in enumerate(shifted)]
    lower = jnp.concatenate(rows + [jnp.zeros((L - COLS, L), F32)], axis=0)
    across = jnp.transpose(lower)
    return [
        jnp.where(lane < (k + 1) * R, rows[k], across[k * R : (k + 1) * R]) for k in range(STEPS + 1)
    ]


def factor(tiles):
    n = len(tiles)
    lane = lax.broadcasted_iota(jnp.int32, (8, L), 1)
    sub = lax.broadcasted_iota(jnp.int32, (8, L), 0)

    def row(value, s):
        return jnp.broadcast_to(value[s : s + 1, :], (8, L))

    triangle, inverse = [], []
    for t in range(n):
        panel = [
            [jnp.broadcast_to(tiles[j][:, 8 * t + c : 8 * t + c + 1], (8, L)) for c in range(8)]
            for j in range(t, n)
        ]
        pivots = None
        for s in range(8):
            here = lane == 8 * t + s
            pivot = row(panel[0][s], s)
            pivots = pivot if s == 0 else jnp.where(sub == s, pivot, pivots)
            one_over = 1.0 / pivot
            scaled = jnp.where(here, 1.0, row(tiles[t], s)) * one_over
            ahead = [row(panel[0][c], s) * one_over for c in range(s + 1, 8)]
            for j in range(t, n):
                factors = panel[j - t][s]
                cleared = here
                if j == t:
                    factors = jnp.where(sub > s, factors, 0.0)
                    cleared = jnp.logical_and(here, sub > s)
                for c in range(s + 1, 8):
                    panel[j - t][c] = panel[j - t][c] - factors * ahead[c - s - 1]
                tiles[j] = jnp.where(cleared, 0.0, tiles[j]) - factors * scaled
        scale = lax.rsqrt(pivots)
        rows = tiles[t] * scale
        index = sub + 8 * t
        triangle.append(jnp.where(lane >= index, rows, 0.0))
        inverse.append(jnp.where(lane < index, rows, jnp.where(lane == index, scale, 0.0)))
    return triangle, inverse


def finish_kernel(g_ref, *refs):
    *blocks, q_ref, r_ref = refs
    tiles = [half for row in unpacked(g_ref) for half in (row[:8], row[8:])]
    triangle, inverse = factor(tiles)
    r_ref[...] = jnp.concatenate(triangle, axis=0)[:, :COLS]
    inverse = jnp.concatenate(inverse, axis=0)[:, :COLS]
    for x in range(2):
        for z in range(Z):
            tall = jnp.concatenate([b[:, lanes(x, z)] for b in blocks], axis=0)
            rows = jnp.transpose(
                jnp.dot(inverse, tall, precision=lax.Precision.HIGHEST, preferred_element_type=F32)
            )
            q_ref[x, 0, z] = rows[:U]
            q_ref[x, 1, z] = rows[U:]


def call(kernel, outs, operands):
    return pl.pallas_call(
        kernel,
        out_shape=[jax.ShapeDtypeStruct(*s) for s in outs],
        in_specs=[VM] * len(operands),
        out_specs=[VM] * len(outs),
        compiler_params=pltpu.CompilerParams(vmem_limit_bytes=VMEM_LIMIT),
    )(*operands)


BLOCK = ((R, WIDE), F32)
PACKETS = [((R, FACE), F32)] * 4
GRAM_ROW = ((R, L), F32)


def exchange(packets):
    wide = lax.axis_size("gx")
    deep = lax.axis_size("gy")

    def even(n):
        return [(i, i ^ 1) for i in range(n)]

    def odd(n):
        there = [(i, (i + 1) % n) for i in range(1, n, 2)]
        return there + [(j, i) for i, j in there]

    e, o, ee, oo = packets
    oo = lax.ppermute(oo, "gy", odd(deep))
    ee = lax.ppermute(ee, "gy", even(deep))
    o = lax.ppermute(o, "gx", odd(wide))
    e = lax.ppermute(e, "gx", even(wide))
    return e, o, ee, oo


GROUPS = ((8, 9, 1), (16 + 8, 48 + 8, 32 + 8), (64 + 8, 192 + 8, 128 + 8), (2 + 8, 6 + 8, 5 + 8))


def total_over_devices(gram):
    axes = ("gx", "gy")
    count = lax.axis_size("gx") * lax.axis_size("gy")
    for masks in GROUPS:
        a, b, c = (lax.ppermute(gram, axes, [(i, i ^ m) for i in range(count)]) for m in masks)
        gram = (gram + a) + (b + c)
    return gram


def first_product(operator_blocks, now):
    local, outer = ((2, Z, L, 3 * L), BF16), ((2, Z, L, L), BF16)
    outs = [local, local, outer, outer, BLOCK, GRAM_ROW]
    return pl.pallas_call(
        first_kernel,
        out_shape=[jax.ShapeDtypeStruct(*s) for s in outs],
        in_specs=[pl.BlockSpec(memory_space=pltpu.HBM), VM],
        out_specs=[VM] * len(outs),
        scratch_shapes=[
            pltpu.VMEM((Z, 2, 2, 7, U, U), F32),
            pltpu.SemaphoreType.DMA((Z,)),
        ],
        compiler_params=pltpu.CompilerParams(vmem_limit_bytes=VMEM_LIMIT),
    )(pltpu.with_memory_space_constraint(operator_blocks, pltpu.HBM), now)


def per_device(operator_blocks, start_block):
    start = jnp.swapaxes(start_block, 3, 4)
    now, *packets = call(begin_kernel, [BLOCK] + PACKETS, [start])
    arrived = exchange(packets)
    *weights, part, row = first_product(operator_blocks, now)
    blocks, rows = [now], [row]
    for step in range(STEPS):
        last = step == STEPS - 1
        if step > 0:
            part, row = call(local_kernel, [BLOCK, GRAM_ROW], [*weights[:2], *blocks])
            rows.append(row)
        new, *packets = call(
            functools.partial(outer_kernel, step),
            [BLOCK] + ([((2 * R, L), F32)] if last else PACKETS),
            [*blocks, *(rows if last else []), part, *arrived, *weights[2:]],
        )
        blocks.append(new)
        if not last:
            arrived = exchange(packets)
    gram = total_over_devices(packets[0])
    outs = [((2, 2, Z, U, COLS), F32), ((COLS, COLS), F32)]
    return call(finish_kernel, outs, [gram, *blocks])


def solution(mesh):
    in_specs = (P("gx", "gy", None, None, None, None), P("gx", "gy", None, None, None))
    out_specs = (P("gx", "gy", None, None, None), P())
    return jax.shard_map(
        per_device, mesh=mesh, in_specs=in_specs, out_specs=out_specs, check_vma=False
    )
```

time: 101 us -> 80.3 us (0.80)
  the two profiles are of different devices: /device:TPU:32 before, /device:TPU:1 now
where the time goes in v1:
time: 80.3 us; the launch traced here: 80.2 us
  starting transfers between devices  42.4 us (53%)
  Pallas kernels  24.7 us (31%)
  waiting for transfers between devices  11.3 us (14%)
  local copies, waits for them, and re-layouts  0.99 us (1%)
    pallas_call x9, Pallas kernels, call(): pl.pallas_call(kernel, out_shape=[jax.ShapeDtypeStruct(*s) for s in outs]...  18.3 us
    ppermute x12, starting transfers between devices, total_over_devices(): lax.ppermute(gram, axes, [(i, i ^ m) for i in range(count)])  17.4 us
    ppermute x4, starting transfers between devices, exchange(): e = lax.ppermute(e, 'gx', even(wide))  14.3 us
    ppermute x4, starting transfers between devices, exchange(): oo = lax.ppermute(oo, 'gy', odd(deep))  8.77 us
    ppermute x12, waiting for transfers between devices, total_over_devices(): lax.ppermute(gram, axes, [(i, i ^ m) for i in range(count)])  8.74 us
    pallas_call x1, Pallas kernels, first_product(): pl.pallas_call(first_kernel, out_shape=[jax.ShapeDtypeStruct(*s) for s in...  6.38 us
    ppermute x4, starting transfers between devices, exchange(): ee = lax.ppermute(ee, 'gy', even(deep))  1.66 us
  transfers between devices with their start and end apart: 28, of which 14 were waited for; matrix products, arithmetic and copies ran while one was open for 0% of the time, Pallas kernels for 17%

profile of v1, /device:TPU:1, one launch (start us, length us, event | category | flops | bytes accessed | tf_op | source)
XLA Modules:
  0.0 80.2 jit_solution(13982045380638680682)
XLA Ops:
  0.6 1.0 %copy-done = f32[2,2,12,64,16]{3,4,2,1,0:T(8,128)S(1)} copy-done((f32[2,2,12,64,16]{3,4,2,1,0:T(8,128)S(1)}, f32[2,2,12,64,16]{3,4,2,1,0:T(8,128)}, u32[]{:S(2)}) %copy-start) | copy-done | bytes 196632
  1.6 0.2 shard_map.41
  1.8 3.3 %collective-permute-start = (f32[16,1536]{1,0:T(8,128)S(1)}, f32[16,1536]{1,0:T(8,128)S(1)}, u32[]{:S(2)}, u32[]{:S(2)}) collective-permute-start(f32[16,1536]{1,0:T(8,128)S(1)} %get-tuple-element.38), channel_id=1, source_target_pairs={{0,8},{8,0},{16,24},{24,16},{32,40},{40,32},{48,56},{56,48},{64,72... | collective-permute-start | bytes 294920 | tf_op jit(solution)/shard_map/ppermute | solution.py:291
  5.1 1.1 %collective-permute-start.2 = (f32[16,1536]{1,0:T(8,128)S(1)}, f32[16,1536]{1,0:T(8,128)S(1)}, u32[]{:S(2)}, u32[]{:S(2)}) collective-permute-start(f32[16,1536]{1,0:T(8,128)S(1)} %get-tuple-element.40), channel_id=1, source_target_pairs={{0,1},{1,0},{2,3},{3,2},{4,5},{5,4},{6,7},{7,6},{8,9},{9,8},{10,11... | collective-permute-start | bytes 294920 | tf_op jit(solution)/shard_map/ppermute | solution.py:289
  6.3 4.7 %collective-permute-start.3 = (f32[16,1536]{1,0:T(8,128)S(1)}, f32[16,1536]{1,0:T(8,128)S(1)}, u32[]{:S(2)}, u32[]{:S(2)}) collective-permute-start(f32[16,1536]{1,0:T(8,128)S(1)} %get-tuple-element.41), channel_id=1, source_target_pairs={{1,2},{3,4},{5,6},{7,0},{2,1},{4,3},{6,5},{0,7},{9,10},{11,12},{13... | collective-permute-start | bytes 294920 | tf_op jit(solution)/shard_map/ppermute | solution.py:288
  10.9 6.4 %shard_map.42 = (bf16[2,12,128,384]{3,2,1,0:T(8,128)(2,1)S(1)}, bf16[2,12,128,384]{3,2,1,0:T(8,128)(2,1)S(1)}, bf16[2,12,128,128]{3,2,1,0:T(8,128)(2,1)S(1)}, bf...) custom-call(f32[2,2,12,7,64,64]{5,4,3,2,1,0:T(8,128)} %a_ref.1, ...), custom_call_target="tpu_custom_call" | custom-call | tf_op jit(solution)/shard_map/pallas_call | solution.py:310
  17.3 1.2 %shard_map.43 = (f32[16,3072]{1,0:T(8,128)S(1)}, f32[16,1536]{1,0:T(8,128)S(1)}, f32[16,1536]{1,0:T(8,128)S(1)}, f32[16,1536]{1,0:T(8,128)S(1)}, f32[16,1536]{1,0:T(8,128)S(1)}) custom-call(f32[16,3072]{1,0:T(8,128)S(1)} %get-tuple-element.36.p_ref.refs_0_, f32[16,3072]{1,0:T(8,128)S(1)} %get-tuple-element.37.refs_1_, ...), custom_call_target="tpu_custom_call" | custom-call | tf_op jit(solution)/shard_map/pallas_call | solution.py:262
  18.5 4.7 %collective-permute-start.4 = (f32[16,1536]{1,0:T(8,128)S(1)}, f32[16,1536]{1,0:T(8,128)S(1)}, u32[]{:S(2)}, u32[]{:S(2)}) collective-permute-start(f32[16,1536]{1,0:T(8,128)S(1)} %get-tuple-element.48), channel_id=1, source_target_pairs={{0,8},{8,0},{16,24},{24,16},{32,40},{40,32},{48,56},{56,48},{64,72... | collective-permute-start | bytes 294920 | tf_op jit(solution)/shard_map/ppermute | solution.py:291
  23.3 1.5 %collective-permute-start.7 = (f32[16,1536]{1,0:T(8,128)S(1)}, f32[16,1536]{1,0:T(8,128)S(1)}, u32[]{:S(2)}, u32[]{:S(2)}) collective-permute-start(f32[16,1536]{1,0:T(8,128)S(1)} %get-tuple-element.51), channel_id=1, source_target_pairs={{1,2},{3,4},{5,6},{7,0},{2,1},{4,3},{6,5},{0,7},{9,10},{11,12},{13... | collective-permute-start | bytes 294920 | tf_op jit(solution)/shard_map/ppermute | solution.py:288
  24.7 2.2 %shard_map.44 = (f32[16,3072]{1,0:T(8,128)S(1)}, f32[16,128]{1,0:T(8,128)S(1)}) custom-call(bf16[2,12,128,384]{3,2,1,0:T(8,128)(2,1)S(1)} %get-tuple-element.45.lh_ref, bf16[2,12,128,384]{3,2,1,0:T(8,128)(2,1)S(1)} %get-tuple-element.46.ll_ref, f32[16,3072]{1,0:T(8,128)S(1)} %get-tuple-element.36.p_ref.refs_0_, f32[16,3072]{1,0:T(8,128)S(1)} %get-tuple-element.44.refs_1_), custom_call_target="tpu_custom_call" | custom-call | tf_op jit(solution)/shard_map/pallas_call | solution.py:262
  27.0 0.0 collective-permute-done.4.refs_3_
  27.0 0.6 collective-permute-done.5.refs_4_
  27.6 0.3 collective-permute-done.7.refs_6_
  27.9 1.2 %shard_map.45 = (f32[16,3072]{1,0:T(8,128)S(1)}, f32[16,1536]{1,0:T(8,128)S(1)}, f32[16,1536]{1,0:T(8,128)S(1)}, f32[16,1536]{1,0:T(8,128)S(1)}, f32[16,1536]{1,0:T(8,128)S(1)}) custom-call(f32[16,3072]{1,0:T(8,128)S(1)} %get-tuple-element.36.p_ref.refs_0_, f32[16,3072]{1,0:T(8,128)S(1)} %get-tuple-element.44.refs_1_, ...), custom_call_target="tpu_custom_call" | custom-call | tf_op jit(solution)/shard_map/pallas_call | solution.py:262
  29.1 2.8 %collective-permute-start.8 = (f32[16,1536]{1,0:T(8,128)S(1)}, f32[16,1536]{1,0:T(8,128)S(1)}, u32[]{:S(2)}, u32[]{:S(2)}) collective-permute-start(f32[16,1536]{1,0:T(8,128)S(1)} %get-tuple-element.54), channel_id=1, source_target_pairs={{0,8},{8,0},{16,24},{24,16},{32,40},{40,32},{48,56},{56,48},{64,72... | collective-permute-start | bytes 294920 | tf_op jit(solution)/shard_map/ppermute | solution.py:291
  31.9 0.2 collective-permute-start.9
  32.2 0.5 collective-permute-start.10
  32.7 1.2 %collective-permute-start.11 = (f32[16,1536]{1,0:T(8,128)S(1)}, f32[16,1536]{1,0:T(8,128)S(1)}, u32[]{:S(2)}, u32[]{:S(2)}) collective-permute-start(f32[16,1536]{1,0:T(8,128)S(1)} %get-tuple-element.57), channel_id=1, source_target_pairs={{1,2},{3,4},{5,6},{7,0},{2,1},{4,3},{6,5},{0,7},{9,10},{11,12},{13... | collective-permute-start | bytes 294920 | tf_op jit(solution)/shard_map/ppermute | solution.py:288
  33.9 2.5 %shard_map.46 = (f32[16,3072]{1,0:T(8,128)S(1)}, f32[16,128]{1,0:T(8,128)S(1)}) custom-call(bf16[2,12,128,384]{3,2,1,0:T(8,128)(2,1)S(1)} %get-tuple-element.45.lh_ref, bf16[2,12,128,384]{3,2,1,0:T(8,128)(2,1)S(1)} %get-tuple-element.46.ll_ref, f32[16,3072]{1,0:T(8,128)S(1)} %get-tuple-element.36.p_ref.refs_0_, f32[16,3072]{1,0:T(8,128)S(1)} %get-tuple-element.44.refs_1_, ...), custom_call_target="tpu_custom_call" | custom-call | tf_op jit(solution)/shard_map/pallas_call | solution.py:262
  36.5 0.9 %collective-permute-done.11.refs_7_ = f32[16,1536]{1,0:T(8,128)S(1)} collective-permute-done((f32[16,1536]{1,0:T(8,128)S(1)}, f32[16,1536]{1,0:T(8,128)S(1)}, u32[]{:S(2)}, u32[]{:S(2)}) %collective-permute-start.11) | collective-permute-done | bytes 98336 | tf_op jit(solution)/shard_map/ppermute | solution.py:288
  37.4 1.2 %shard_map.47 = (f32[16,3072]{1,0:T(8,128)S(1)}, f32[16,1536]{1,0:T(8,128)S(1)}, f32[16,1536]{1,0:T(8,128)S(1)}, f32[16,1536]{1,0:T(8,128)S(1)}, f32[16,1536]{1,0:T(8,128)S(1)}) custom-call(f32[16,3072]{1,0:T(8,128)S(1)} %get-tuple-element.36.p_ref.refs_0_, f32[16,3072]{1,0:T(8,128)S(1)} %get-tuple-element.44.refs_1_, ...), custom_call_target="tpu_custom_call" | custom-call | tf_op jit(solution)/shard_map/pallas_call | solution.py:262
  38.5 3.5 %collective-permute-start.12 = (f32[16,1536]{1,0:T(8,128)S(1)}, f32[16,1536]{1,0:T(8,128)S(1)}, u32[]{:S(2)}, u32[]{:S(2)}) collective-permute-start(f32[16,1536]{1,0:T(8,128)S(1)} %get-tuple-element.64), channel_id=1, source_target_pairs={{0,8},{8,0},{16,24},{24,16},{32,40},{40,32},{48,56},{56,48},{64,72... | collective-permute-start | bytes 294920 | tf_op jit(solution)/shard_map/ppermute | solution.py:291
  42.0 1.5 %collective-permute-start.15 = (f32[16,1536]{1,0:T(8,128)S(1)}, f32[16,1536]{1,0:T(8,128)S(1)}, u32[]{:S(2)}, u32[]{:S(2)}) collective-permute-start(f32[16,1536]{1,0:T(8,128)S(1)} %get-tuple-element.67), channel_id=1, source_target_pairs={{1,2},{3,4},{5,6},{7,0},{2,1},{4,3},{6,5},{0,7},{9,10},{11,12},{13... | collective-permute-start | bytes 294920 | tf_op jit(solution)/shard_map/ppermute | solution.py:288
  43.5 2.5 %shard_map.48 = (f32[16,3072]{1,0:T(8,128)S(1)}, f32[16,128]{1,0:T(8,128)S(1)}) custom-call(bf16[2,12,128,384]{3,2,1,0:T(8,128)(2,1)S(1)} %get-tuple-element.45.lh_ref, bf16[2,12,128,384]{3,2,1,0:T(8,128)(2,1)S(1)} %get-tuple-element.46.ll_ref, f32[16,3072]{1,0:T(8,128)S(1)} %get-tuple-element.36.p_ref.refs_0_, f32[16,3072]{1,0:T(8,128)S(1)} %get-tuple-element.44.refs_1_, ...), custom_call_target="tpu_custom_call" | custom-call | tf_op jit(solution)/shard_map/pallas_call | solution.py:262
  46.0 0.0 collective-permute-done.12.refs_9_
  46.0 0.3 collective-permute-done.13.refs_10_
  46.3 0.3 collective-permute-done.15.refs_12_
  46.7 2.6 %shard_map.49 = (f32[16,3072]{1,0:T(8,128)S(1)}, f32[32,128]{1,0:T(8,128)S(1)}) custom-call(f32[16,3072]{1,0:T(8,128)S(1)} %get-tuple-element.36.p_ref.refs_0_, f32[16,3072]{1,0:T(8,128)S(1)} %get-tuple-element.44.refs_1_, f32[16,3072]{1,0:T(8,128)S(1)} %get-tuple-element.52.refs_2_, f32[16,3072]{1,0:T(8,128)S(1)} %get-tuple-element.58.refs_3_, ...), custom_call_target="tpu_custom_call" | custom-call | tf_op jit(solution)/shard_map/pallas_call | solution.py:262
  49.3 0.6 collective-permute-start.18
  49.9 3.9 %collective-permute-start.17 = (f32[32,128]{1,0:T(8,128)S(1)}, f32[32,128]{1,0:T(8,128)S(1)}, u32[]{:S(2)}, u32[]{:S(2)}) collective-permute-start(f32[32,128]{1,0:T(8,128)S(1)} %get-tuple-element.68), channel_id=1, source_target_pairs={{0,9},{1,8},{2,11},{3,10},{4,13},{5,12},{6,15},{7,14},{8,1},{9,0},... | collective-permute-start | bytes 49160 | tf_op jit(solution)/shard_map/ppermute | solution.py:302
  53.7 1.7 %collective-permute-done.17 = f32[32,128]{1,0:T(8,128)S(1)} collective-permute-done((f32[32,128]{1,0:T(8,128)S(1)}, f32[32,128]{1,0:T(8,128)S(1)}, u32[]{:S(2)}, u32[]{:S(2)}) %collective-permute-start.17) | collective-permute-done | bytes 16416 | tf_op jit(solution)/shard_map/ppermute | solution.py:302
  55.4 0.6 collective-permute-start.21
  56.0 2.8 %collective-permute-start.20 = (f32[32,128]{1,0:T(8,128)S(1)}, f32[32,128]{1,0:T(8,128)S(1)}, u32[]{:S(2)}, u32[]{:S(2)}) collective-permute-start(f32[32,128]{1,0:T(8,128)S(1)} %add_add_fusion.3), channel_id=1, source_target_pairs={{0,56},{1,57},{2,58},{3,59},{4,60},{5,61},{6,62},{7,63},{8,48},{9,... | collective-permute-start | bytes 49160 | tf_op jit(solution)/shard_map/ppermute | solution.py:302
  58.8 1.4 %collective-permute-done.21 = f32[32,128]{1,0:T(8,128)S(1)} collective-permute-done((f32[32,128]{1,0:T(8,128)S(1)}, f32[32,128]{1,0:T(8,128)S(1)}, u32[]{:S(2)}, u32[]{:S(2)}) %collective-permute-start.21) | collective-permute-done | bytes 16416 | tf_op jit(solution)/shard_map/ppermute | solution.py:302
  60.2 0.4 collective-permute-done.20
  60.6 1.4 %collective-permute-done.19 = f32[32,128]{1,0:T(8,128)S(1)} collective-permute-done((f32[32,128]{1,0:T(8,128)S(1)}, f32[32,128]{1,0:T(8,128)S(1)}, u32[]{:S(2)}, u32[]{:S(2)}) %collective-permute-start.19) | collective-permute-done | bytes 16416 | tf_op jit(solution)/shard_map/ppermute | solution.py:302
  62.0 0.3 collective-permute-start.24
  62.3 0.2 collective-permute-start.23
  62.5 3.0 %collective-permute-start.22 = (f32[32,128]{1,0:T(8,128)S(1)}, f32[32,128]{1,0:T(8,128)S(1)}, u32[]{:S(2)}, u32[]{:S(2)}) collective-permute-start(f32[32,128]{1,0:T(8,128)S(1)} %add_add_fusion.2), channel_id=1, source_target_pairs={{0,72},{1,73},{2,74},{3,75},{4,76},{5,77},{6,78},{7,79},{8,64},{9,... | collective-permute-start | bytes 49160 | tf_op jit(solution)/shard_map/ppermute | solution.py:302
  65.5 1.5 %collective-permute-done.24 = f32[32,128]{1,0:T(8,128)S(1)} collective-permute-done((f32[32,128]{1,0:T(8,128)S(1)}, f32[32,128]{1,0:T(8,128)S(1)}, u32[]{:S(2)}, u32[]{:S(2)}) %collective-permute-start.24) | collective-permute-done | bytes 16416 | tf_op jit(solution)/shard_map/ppermute | solution.py:302
  67.0 0.1 collective-permute-done.23
  67.1 3.0 %collective-permute-start.27 = (f32[32,128]{1,0:T(8,128)S(1)}, f32[32,128]{1,0:T(8,128)S(1)}, u32[]{:S(2)}, u32[]{:S(2)}) collective-permute-start(f32[32,128]{1,0:T(8,128)S(1)} %add_add_fusion.1), channel_id=1, source_target_pairs={{0,13},{1,12},{2,15},{3,14},{4,9},{5,8},{6,11},{7,10},{8,5},{9,4},... | collective-permute-start | bytes 49160 | tf_op jit(solution)/shard_map/ppermute | solution.py:302
  70.0 1.4 %collective-permute-start.26 = (f32[32,128]{1,0:T(8,128)S(1)}, f32[32,128]{1,0:T(8,128)S(1)}, u32[]{:S(2)}, u32[]{:S(2)}) collective-permute-start(f32[32,128]{1,0:T(8,128)S(1)} %add_add_fusion.1), channel_id=1, source_target_pairs={{0,14},{1,15},{2,12},{3,13},{4,10},{5,11},{6,8},{7,9},{8,6},{9,7},... | collective-permute-start | bytes 49160 | tf_op jit(solution)/shard_map/ppermute | solution.py:302
  71.4 1.7 %collective-permute-start.25 = (f32[32,128]{1,0:T(8,128)S(1)}, f32[32,128]{1,0:T(8,128)S(1)}, u32[]{:S(2)}, u32[]{:S(2)}) collective-permute-start(f32[32,128]{1,0:T(8,128)S(1)} %add_add_fusion.1), channel_id=1, source_target_pairs={{0,10},{1,11},{2,8},{3,9},{4,14},{5,15},{6,12},{7,13},{8,2},{9,3},... | collective-permute-start | bytes 49160 | tf_op jit(solution)/shard_map/ppermute | solution.py:302
  73.2 0.2 collective-permute-done.27
  73.3 2.0 %collective-permute-done.26 = f32[32,128]{1,0:T(8,128)S(1)} collective-permute-done((f32[32,128]{1,0:T(8,128)S(1)}, f32[32,128]{1,0:T(8,128)S(1)}, u32[]{:S(2)}, u32[]{:S(2)}) %collective-permute-start.26) | collective-permute-done | bytes 16416 | tf_op jit(solution)/shard_map/ppermute | solution.py:302
  75.3 0.2 collective-permute-done.25
  75.5 4.6 %shard_map.50 = (f32[2,2,12,64,80]{4,3,2,1,0:T(8,128)}, f32[80,80]{1,0:T(8,128)}) custom-call(f32[32,128]{1,0:T(8,128)S(1)} %add_add_fusion.g_ref, f32[16,3072]{1,0:T(8,128)S(1)} %get-tuple-element.36.p_ref.refs_0_, f32[16,3072]{1,0:T(8,128)S(1)} %get-tuple-element.44.refs_1_, f32[16,3072]{1,0:T(8,128)S(1)} %get-tuple-element.52.refs_2_, ...), custom_call_target="tpu_custom_call" | custom-call | tf_op jit(solution)/shard_map/pallas_call | solution.py:262
  (24 shorter events, 0.1 us)
Async XLA Ops:
  0.6 1.0 %copy-start = (f32[2,2,12,64,16]{3,4,2,1,0:T(8,128)S(1)}, f32[2,2,12,64,16]{3,4,2,1,0:T(8,128)}, u32[]{:S(2)}) copy-start(f32[2,2,12,64,16]{3,4,2,1,0:T(8,128)} %param.3) | copy-start | bytes 589828
  1.8 15.5 %collective-permute-start = (f32[16,1536]{1,0:T(8,128)S(1)}, f32[16,1536]{1,0:T(8,128)S(1)}, u32[]{:S(2)}, u32[]{:S(2)}) collective-permute-start(f32[16,1536]{1,0:T(8,128)S(1)} %get-tuple-element.38), channel_id=1, source_target_pairs={{0,8},{8,0},{16,24},{24,16},{32,40},{40,32},{48,56},{56,48},{64,72... | collective-permute-start | bytes 294920 | tf_op jit(solution)/shard_map/ppermute | solution.py:291
  5.1 12.2 %collective-permute-start.1 = (f32[16,1536]{1,0:T(8,128)S(1)}, f32[16,1536]{1,0:T(8,128)S(1)}, u32[]{:S(2)}, u32[]{:S(2)}) collective-permute-start(f32[16,1536]{1,0:T(8,128)S(1)} %get-tuple-element.39), channel_id=1, source_target_pairs={{8,16},{24,32},{40,48},{56,64},{72,80},{88,96},{104,112},{120,128}... | collective-permute-start | bytes 294920 | tf_op jit(solution)/shard_map/ppermute | solution.py:290
  5.1 12.2 %collective-permute-start.2 = (f32[16,1536]{1,0:T(8,128)S(1)}, f32[16,1536]{1,0:T(8,128)S(1)}, u32[]{:S(2)}, u32[]{:S(2)}) collective-permute-start(f32[16,1536]{1,0:T(8,128)S(1)} %get-tuple-element.40), channel_id=1, source_target_pairs={{0,1},{1,0},{2,3},{3,2},{4,5},{5,4},{6,7},{7,6},{8,9},{9,8},{10,11... | collective-permute-start | bytes 294920 | tf_op jit(solution)/shard_map/ppermute | solution.py:289
  6.3 11.1 %collective-permute-start.3 = (f32[16,1536]{1,0:T(8,128)S(1)}, f32[16,1536]{1,0:T(8,128)S(1)}, u32[]{:S(2)}, u32[]{:S(2)}) collective-permute-start(f32[16,1536]{1,0:T(8,128)S(1)} %get-tuple-element.41), channel_id=1, source_target_pairs={{1,2},{3,4},{5,6},{7,0},{2,1},{4,3},{6,5},{0,7},{9,10},{11,12},{13... | collective-permute-start | bytes 294920 | tf_op jit(solution)/shard_map/ppermute | solution.py:288
  18.5 8.4 %collective-permute-start.4 = (f32[16,1536]{1,0:T(8,128)S(1)}, f32[16,1536]{1,0:T(8,128)S(1)}, u32[]{:S(2)}, u32[]{:S(2)}) collective-permute-start(f32[16,1536]{1,0:T(8,128)S(1)} %get-tuple-element.48), channel_id=1, source_target_pairs={{0,8},{8,0},{16,24},{24,16},{32,40},{40,32},{48,56},{56,48},{64,72... | collective-permute-start | bytes 294920 | tf_op jit(solution)/shard_map/ppermute | solution.py:291
  23.3 4.3 %collective-permute-start.5 = (f32[16,1536]{1,0:T(8,128)S(1)}, f32[16,1536]{1,0:T(8,128)S(1)}, u32[]{:S(2)}, u32[]{:S(2)}) collective-permute-start(f32[16,1536]{1,0:T(8,128)S(1)} %get-tuple-element.49), channel_id=1, source_target_pairs={{8,16},{24,32},{40,48},{56,64},{72,80},{88,96},{104,112},{120,128}... | collective-permute-start | bytes 294920 | tf_op jit(solution)/shard_map/ppermute | solution.py:290
  23.3 4.3 %collective-permute-start.6 = (f32[16,1536]{1,0:T(8,128)S(1)}, f32[16,1536]{1,0:T(8,128)S(1)}, u32[]{:S(2)}, u32[]{:S(2)}) collective-permute-start(f32[16,1536]{1,0:T(8,128)S(1)} %get-tuple-element.50), channel_id=1, source_target_pairs={{0,1},{1,0},{2,3},{3,2},{4,5},{5,4},{6,7},{7,6},{8,9},{9,8},{10,11... | collective-permute-start | bytes 294920 | tf_op jit(solution)/shard_map/ppermute | solution.py:289
  23.3 4.7 %collective-permute-start.7 = (f32[16,1536]{1,0:T(8,128)S(1)}, f32[16,1536]{1,0:T(8,128)S(1)}, u32[]{:S(2)}, u32[]{:S(2)}) collective-permute-start(f32[16,1536]{1,0:T(8,128)S(1)} %get-tuple-element.51), channel_id=1, source_target_pairs={{1,2},{3,4},{5,6},{7,0},{2,1},{4,3},{6,5},{0,7},{9,10},{11,12},{13... | collective-permute-start | bytes 294920 | tf_op jit(solution)/shard_map/ppermute | solution.py:288
  29.1 7.3 %collective-permute-start.8 = (f32[16,1536]{1,0:T(8,128)S(1)}, f32[16,1536]{1,0:T(8,128)S(1)}, u32[]{:S(2)}, u32[]{:S(2)}) collective-permute-start(f32[16,1536]{1,0:T(8,128)S(1)} %get-tuple-element.54), channel_id=1, source_target_pairs={{0,8},{8,0},{16,24},{24,16},{32,40},{40,32},{48,56},{56,48},{64,72... | collective-permute-start | bytes 294920 | tf_op jit(solution)/shard_map/ppermute | solution.py:291
  31.9 4.5 %collective-permute-start.9 = (f32[16,1536]{1,0:T(8,128)S(1)}, f32[16,1536]{1,0:T(8,128)S(1)}, u32[]{:S(2)}, u32[]{:S(2)}) collective-permute-start(f32[16,1536]{1,0:T(8,128)S(1)} %get-tuple-element.55), channel_id=1, source_target_pairs={{8,16},{24,32},{40,48},{56,64},{72,80},{88,96},{104,112},{120,128}... | collective-permute-start | bytes 294920 | tf_op jit(solution)/shard_map/ppermute | solution.py:290
  32.2 4.3 %collective-permute-start.10 = (f32[16,1536]{1,0:T(8,128)S(1)}, f32[16,1536]{1,0:T(8,128)S(1)}, u32[]{:S(2)}, u32[]{:S(2)}) collective-permute-start(f32[16,1536]{1,0:T(8,128)S(1)} %get-tuple-element.56), channel_id=1, source_target_pairs={{0,1},{1,0},{2,3},{3,2},{4,5},{5,4},{6,7},{7,6},{8,9},{9,8},{10,11... | collective-permute-start | bytes 294920 | tf_op jit(solution)/shard_map/ppermute | solution.py:289
  32.7 4.7 %collective-permute-start.11 = (f32[16,1536]{1,0:T(8,128)S(1)}, f32[16,1536]{1,0:T(8,128)S(1)}, u32[]{:S(2)}, u32[]{:S(2)}) collective-permute-start(f32[16,1536]{1,0:T(8,128)S(1)} %get-tuple-element.57), channel_id=1, source_target_pairs={{1,2},{3,4},{5,6},{7,0},{2,1},{4,3},{6,5},{0,7},{9,10},{11,12},{13... | collective-permute-start | bytes 294920 | tf_op jit(solution)/shard_map/ppermute | solution.py:288
  38.5 7.4 %collective-permute-start.12 = (f32[16,1536]{1,0:T(8,128)S(1)}, f32[16,1536]{1,0:T(8,128)S(1)}, u32[]{:S(2)}, u32[]{:S(2)}) collective-permute-start(f32[16,1536]{1,0:T(8,128)S(1)} %get-tuple-element.64), channel_id=1, source_target_pairs={{0,8},{8,0},{16,24},{24,16},{32,40},{40,32},{48,56},{56,48},{64,72... | collective-permute-start | bytes 294920 | tf_op jit(solution)/shard_map/ppermute | solution.py:291
  42.0 4.3 %collective-permute-start.13 = (f32[16,1536]{1,0:T(8,128)S(1)}, f32[16,1536]{1,0:T(8,128)S(1)}, u32[]{:S(2)}, u32[]{:S(2)}) collective-permute-start(f32[16,1536]{1,0:T(8,128)S(1)} %get-tuple-element.65), channel_id=1, source_target_pairs={{8,16},{24,32},{40,48},{56,64},{72,80},{88,96},{104,112},{120,128}... | collective-permute-start | bytes 294920 | tf_op jit(solution)/shard_map/ppermute | solution.py:290
  42.0 4.3 %collective-permute-start.14 = (f32[16,1536]{1,0:T(8,128)S(1)}, f32[16,1536]{1,0:T(8,128)S(1)}, u32[]{:S(2)}, u32[]{:S(2)}) collective-permute-start(f32[16,1536]{1,0:T(8,128)S(1)} %get-tuple-element.66), channel_id=1, source_target_pairs={{0,1},{1,0},{2,3},{3,2},{4,5},{5,4},{6,7},{7,6},{8,9},{9,8},{10,11... | collective-permute-start | bytes 294920 | tf_op jit(solution)/shard_map/ppermute | solution.py:289
  42.0 4.7 %collective-permute-start.15 = (f32[16,1536]{1,0:T(8,128)S(1)}, f32[16,1536]{1,0:T(8,128)S(1)}, u32[]{:S(2)}, u32[]{:S(2)}) collective-permute-start(f32[16,1536]{1,0:T(8,128)S(1)} %get-tuple-element.67), channel_id=1, source_target_pairs={{1,2},{3,4},{5,6},{7,0},{2,1},{4,3},{6,5},{0,7},{9,10},{11,12},{13... | collective-permute-start | bytes 294920 | tf_op jit(solution)/shard_map/ppermute | solution.py:288
  49.3 4.4 %collective-permute-start.18 = (f32[32,128]{1,0:T(8,128)S(1)}, f32[32,128]{1,0:T(8,128)S(1)}, u32[]{:S(2)}, u32[]{:S(2)}) collective-permute-start(f32[32,128]{1,0:T(8,128)S(1)} %get-tuple-element.68), channel_id=1, source_target_pairs={{0,1},{1,0},{2,3},{3,2},{4,5},{5,4},{6,7},{7,6},{8,9},{9,8},{10,11... | collective-permute-start | bytes 49160 | tf_op jit(solution)/shard_map/ppermute | solution.py:302
  49.9 5.6 %collective-permute-start.17 = (f32[32,128]{1,0:T(8,128)S(1)}, f32[32,128]{1,0:T(8,128)S(1)}, u32[]{:S(2)}, u32[]{:S(2)}) collective-permute-start(f32[32,128]{1,0:T(8,128)S(1)} %get-tuple-element.68), channel_id=1, source_target_pairs={{0,9},{1,8},{2,11},{3,10},{4,13},{5,12},{6,15},{7,14},{8,1},{9,0},... | collective-permute-start | bytes 49160 | tf_op jit(solution)/shard_map/ppermute | solution.py:302
  53.7 1.7 %collective-permute-start.16 = (f32[32,128]{1,0:T(8,128)S(1)}, f32[32,128]{1,0:T(8,128)S(1)}, u32[]{:S(2)}, u32[]{:S(2)}) collective-permute-start(f32[32,128]{1,0:T(8,128)S(1)} %get-tuple-element.68), channel_id=1, source_target_pairs={{0,8},{1,9},{2,10},{3,11},{4,12},{5,13},{6,14},{7,15},{8,0},{9,1},... | collective-permute-start | bytes 49160 | tf_op jit(solution)/shard_map/ppermute | solution.py:302
  55.4 4.8 %collective-permute-start.21 = (f32[32,128]{1,0:T(8,128)S(1)}, f32[32,128]{1,0:T(8,128)S(1)}, u32[]{:S(2)}, u32[]{:S(2)}) collective-permute-start(f32[32,128]{1,0:T(8,128)S(1)} %add_add_fusion.3), channel_id=1, source_target_pairs={{0,40},{1,41},{2,42},{3,43},{4,44},{5,45},{6,46},{7,47},{8,32},{9,... | collective-permute-start | bytes 49160 | tf_op jit(solution)/shard_map/ppermute | solution.py:302
  56.0 4.6 %collective-permute-start.20 = (f32[32,128]{1,0:T(8,128)S(1)}, f32[32,128]{1,0:T(8,128)S(1)}, u32[]{:S(2)}, u32[]{:S(2)}) collective-permute-start(f32[32,128]{1,0:T(8,128)S(1)} %add_add_fusion.3), channel_id=1, source_target_pairs={{0,56},{1,57},{2,58},{3,59},{4,60},{5,61},{6,62},{7,63},{8,48},{9,... | collective-permute-start | bytes 49160 | tf_op jit(solution)/shard_map/ppermute | solution.py:302
  58.8 3.2 %collective-permute-start.19 = (f32[32,128]{1,0:T(8,128)S(1)}, f32[32,128]{1,0:T(8,128)S(1)}, u32[]{:S(2)}, u32[]{:S(2)}) collective-permute-start(f32[32,128]{1,0:T(8,128)S(1)} %add_add_fusion.3), channel_id=1, source_target_pairs={{0,24},{1,25},{2,26},{3,27},{4,28},{5,29},{6,30},{7,31},{8,16},{9,... | collective-permute-start | bytes 49160 | tf_op jit(solution)/shard_map/ppermute | solution.py:302
  62.0 5.0 %collective-permute-start.24 = (f32[32,128]{1,0:T(8,128)S(1)}, f32[32,128]{1,0:T(8,128)S(1)}, u32[]{:S(2)}, u32[]{:S(2)}) collective-permute-start(f32[32,128]{1,0:T(8,128)S(1)} %add_add_fusion.2), channel_id=1, source_target_pairs={{0,136},{1,137},{2,138},{3,139},{4,140},{5,141},{6,142},{7,143},{8... | collective-permute-start | bytes 49160 | tf_op jit(solution)/shard_map/ppermute | solution.py:302
  62.3 4.7 %collective-permute-start.23 = (f32[32,128]{1,0:T(8,128)S(1)}, f32[32,128]{1,0:T(8,128)S(1)}, u32[]{:S(2)}, u32[]{:S(2)}) collective-permute-start(f32[32,128]{1,0:T(8,128)S(1)} %add_add_fusion.2), channel_id=1, source_target_pairs={{0,200},{1,201},{2,202},{3,203},{4,204},{5,205},{6,206},{7,207},{8... | collective-permute-start | bytes 49160 | tf_op jit(solution)/shard_map/ppermute | solution.py:302
  62.5 4.5 %collective-permute-start.22 = (f32[32,128]{1,0:T(8,128)S(1)}, f32[32,128]{1,0:T(8,128)S(1)}, u32[]{:S(2)}, u32[]{:S(2)}) collective-permute-start(f32[32,128]{1,0:T(8,128)S(1)} %add_add_fusion.2), channel_id=1, source_target_pairs={{0,72},{1,73},{2,74},{3,75},{4,76},{5,77},{6,78},{7,79},{8,64},{9,... | collective-permute-start | bytes 49160 | tf_op jit(solution)/shard_map/ppermute | solution.py:302
  67.1 6.3 %collective-permute-start.27 = (f32[32,128]{1,0:T(8,128)S(1)}, f32[32,128]{1,0:T(8,128)S(1)}, u32[]{:S(2)}, u32[]{:S(2)}) collective-permute-start(f32[32,128]{1,0:T(8,128)S(1)} %add_add_fusion.1), channel_id=1, source_target_pairs={{0,13},{1,12},{2,15},{3,14},{4,9},{5,8},{6,11},{7,10},{8,5},{9,4},... | collective-permute-start | bytes 49160 | tf_op jit(solution)/shard_map/ppermute | solution.py:302
  70.0 5.3 %collective-permute-start.26 = (f32[32,128]{1,0:T(8,128)S(1)}, f32[32,128]{1,0:T(8,128)S(1)}, u32[]{:S(2)}, u32[]{:S(2)}) collective-permute-start(f32[32,128]{1,0:T(8,128)S(1)} %add_add_fusion.1), channel_id=1, source_target_pairs={{0,14},{1,15},{2,12},{3,13},{4,10},{5,11},{6,8},{7,9},{8,6},{9,7},... | collective-permute-start | bytes 49160 | tf_op jit(solution)/shard_map/ppermute | solution.py:302
  71.4 4.1 %collective-permute-start.25 = (f32[32,128]{1,0:T(8,128)S(1)}, f32[32,128]{1,0:T(8,128)S(1)}, u32[]{:S(2)}, u32[]{:S(2)}) collective-permute-start(f32[32,128]{1,0:T(8,128)S(1)} %add_add_fusion.1), channel_id=1, source_target_pairs={{0,10},{1,11},{2,8},{3,9},{4,14},{5,15},{6,12},{7,13},{8,2},{9,3},... | collective-permute-start | bytes 49160 | tf_op jit(solution)/shard_map/ppermute | solution.py:302

commit v2 on v1

v2 whole, which is shorter than its diff:
```python
import functools

import jax
import jax.numpy as jnp
from jax import lax
from jax.experimental import pallas as pl
from jax.experimental.pallas import tpu as pltpu
from jax.sharding import PartitionSpec as P


F32 = jnp.float32
BF16 = jnp.bfloat16
Z = 12
R = 16
U = 64
L = 2 * U
FACE = Z * L
WIDE = 2 * FACE
STEPS = 4
COLS = (STEPS + 1) * R
VMEM_LIMIT = 16 * 1024 * 1024
NT = (((1,), (1,)), ((), ()))

VM = pl.BlockSpec(memory_space=pltpu.VMEM)


def low_lanes(shape):
    return lax.broadcasted_iota(jnp.int32, shape, len(shape) - 1) < U


def split(value):
    high = value.astype(BF16)
    return high, (value - high.astype(F32)).astype(BF16)


def product(high, low, weights):
    left = jnp.concatenate([high, low], axis=0)
    both = lax.dot_general(
        jnp.concatenate([left, left], axis=1), weights, NT, preferred_element_type=F32
    )
    return both[:R] + both[R:]


def swapped(pair):
    return pltpu.roll(pair, U, 1)


def parity():
    return lax.axis_index("gx") & 1, lax.axis_index("gy") & 1


def lanes(x, z):
    base = (x * Z + z) * L
    return slice(base, base + L)


def store_packets(pairs, px, py, e_ref, o_ref, ee_ref, oo_ref):
    low = low_lanes((R, L))
    for z in range(Z):
        at = slice(z * L, (z + 1) * L)
        first, second = pairs[0][z], pairs[1][z]
        e_ref[:, at] = jnp.where(px == 0, second, first)
        o_ref[:, at] = jnp.where(px == 0, first, second)
        turned = swapped(first)
        face0 = jnp.where(low, second, turned)
        face1 = jnp.where(low, turned, second)
        ee_ref[:, at] = jnp.where(py == 0, face1, face0)
        oo_ref[:, at] = jnp.where(py == 0, face0, face1)


def begin_kernel(s_ref, p_ref, h_ref, l_ref, e_ref, o_ref, ee_ref, oo_ref):
    px, py = parity()
    pairs = [[None] * Z for _ in range(2)]
    for x in range(2):
        for z in range(Z):
            pair = jnp.concatenate([s_ref[x, 0, z], s_ref[x, 1, z]], axis=1)
            p_ref[:, lanes(x, z)] = pair
            h_ref[:, lanes(x, z)], l_ref[:, lanes(x, z)] = split(pair)
            pairs[x][z] = pair
    store_packets(pairs, px, py, e_ref, o_ref, ee_ref, oo_ref)


def local_pair(h_ref, l_ref, w_ref, x, z):
    def rows(ref):
        zero = jnp.zeros((R, L), BF16)
        below = ref[:, lanes(x, z - 1)] if z > 0 else zero
        above = ref[:, lanes(x, z + 1)] if z < Z - 1 else zero
        return jnp.concatenate([ref[:, lanes(x, z)], ref[:, lanes(1 - x, z)], below, above], axis=1)

    return product(rows(h_ref), rows(l_ref), w_ref[x, z])


def gram_row(highs, lows):
    newest = jnp.concatenate([highs[-1], lows[-1]], axis=0)
    both = lax.dot_general(
        newest, jnp.concatenate(highs, axis=0), NT, preferred_element_type=F32
    ) + lax.dot_general(newest, jnp.concatenate(lows, axis=0), NT, preferred_element_type=F32)
    row = both[:R] + both[R:]
    return jnp.concatenate([row, jnp.zeros((R, L - row.shape[1]), F32)], axis=1)


CHUNK = 2
TILES = 4
OUTER = 2


def first_kernel(a_ref, h_ref, l_ref, w_ref, v_ref, out_ref, buffer, arrived):
    copies = [
        pltpu.make_async_copy(
            a_ref.at[:, :, pl.ds(z, CHUNK)], buffer.at[:, :, pl.ds(z, CHUNK)], arrived.at[z]
        )
        for z in range(0, Z, CHUNK)
    ]
    for copy in copies:
        copy.start()
    for x in range(2):
        for z in range(Z):
            for k in range(2):
                w_ref[x, z, :, (k * TILES + 1) * L : (k + 1) * TILES * L] = jnp.zeros(
                    (L, (TILES - 1) * L), BF16
                )
            v_ref[x, z] = jnp.zeros((L, 2 * OUTER * L), BF16)

    def store(ref, x, z, rows, tile, tiles, halves, at=slice(0, L)):
        for k, half in enumerate(halves):
            base = (k * tiles + tile) * L
            ref[x, z, rows, base + at.start : base + at.stop] = half[:, at]

    def multiply(chunk):
        for z in chunk:
            for x in range(2):
                out_ref[:, lanes(x, z)] = local_pair(h_ref, l_ref, w_ref, x, z)

    behind = ()
    for z0, copy in zip(range(0, Z, CHUNK), copies):
        copy.wait()
        chunk = range(z0, z0 + CHUNK)
        for z in chunk:
            for x in range(2):
                rows = (slice(0, U), slice(U, L))

                def block(y, f):
                    return buffer[x, y, z, f]

                def beside(one, two):
                    return split(jnp.concatenate([one, two], axis=1))

                store(w_ref, x, z, rows[0], 0, TILES, beside(block(0, 0), block(0, 4)))
                store(w_ref, x, z, rows[1], 0, TILES, beside(block(1, 3), block(1, 0)))
                apart = [
                    (w_ref, 1, TILES, 2 - x, 2 - x),
                    (w_ref, 2, TILES, 5, 5),
                    (w_ref, 3, TILES, 6, 6),
                    (v_ref, 0, OUTER, 1 + x, 1 + x),
                    (v_ref, 1, OUTER, 3, 4),
                ]
                for ref, tile, tiles, fa, fb in apart:
                    turn = x if ref is v_ref and tile == 1 else 0
                    one, two = block(0, fa), block(1, fb)
                    halves = beside(two, one) if turn else beside(one, two)
                    store(ref, x, z, rows[turn], tile, tiles, halves, rows[0])
                    store(ref, x, z, rows[1 - turn], tile, tiles, halves, rows[1])
        multiply(behind)
        behind = chunk
    multiply(behind)


def local_kernel(step, w_ref, *refs):
    highs, lows = refs[: step + 1], refs[step + 1 : 2 * step + 2]
    out_ref, *rows = refs[2 * step + 2 :]
    if step == 1:
        rows[0][...] = gram_row([h[...] for h in highs[:1]], [l[...] for l in lows[:1]])
    rows[-1][...] = gram_row([h[...] for h in highs], [l[...] for l in lows])
    for z in range(Z):
        for x in range(2):
            out_ref[:, lanes(x, z)] = local_pair(highs[-1], lows[-1], w_ref, x, z)


def outer_kernel(step, *refs):
    first, last = step == 0, step == STEPS - 1
    now_ref, refs = refs[0], refs[1:]
    if not first:
        before_ref, refs = refs[0], refs[1:]
    if last:
        rows, highs, lows = refs[:STEPS], refs[STEPS : 2 * STEPS], refs[2 * STEPS : 3 * STEPS]
        refs = refs[3 * STEPS :]
    part_ref, e_ref, o_ref, ee_ref, oo_ref, v_ref, *outs = refs
    high_ref, low_ref, *outs = outs
    px, py = parity()
    low = low_lanes((R, L))
    gx, gy = lax.axis_index("gx"), lax.axis_index("gy")
    o_there = jnp.logical_and(gx > 0, gx < lax.axis_size("gx") - 1)
    oo_there = jnp.logical_and(gy > 0, gy < lax.axis_size("gy") - 1)
    pairs, sums = [[None] * Z for _ in range(2)], []
    for z in range(Z):
        at = slice(z * L, (z + 1) * L)
        e, o, ee, oo = e_ref[:, at], o_ref[:, at], ee_ref[:, at], oo_ref[:, at]
        o = jnp.where(o_there, o, 0.0)
        oo = jnp.where(oo_there, oo, 0.0)
        x0, x1 = jnp.where(px == 0, o, e), jnp.where(px == 0, e, o)
        ym, yp = jnp.where(py == 0, oo, ee), jnp.where(py == 0, ee, oo)
        beyond = ((x0, jnp.where(low, ym, yp)), (x1, jnp.where(low, yp, ym)))
        for x, left in enumerate(beyond):
            here = lanes(x, z)
            high, less = split(jnp.concatenate(left, axis=1))
            applied = part_ref[:, here] + product(high, less, v_ref[x, z])
            shifted = (applied - 8.0 * now_ref[:, here]) * (1.0 / 6.0)
            pairs[x][z] = shifted if first else 2.0 * shifted - before_ref[:, here]
            high_ref[:, here], low_ref[:, here] = split(pairs[x][z])
            if not last:
                outs[0][:, here] = pairs[x][z]
            else:
                newest = [high_ref[:, here], low_ref[:, here]]
                every = [h[:, here] for h in highs] + newest[:1] + [l[:, here] for l in lows] + newest[1:]
                sums.append((jnp.concatenate(newest, axis=0), jnp.concatenate(every, axis=0)))
    if not last:
        store_packets(pairs, px, py, *outs[1:])
        return
    both = jnp.zeros((2 * R, 2 * COLS), F32)
    for one, two in zip(sums[::2], sums[1::2]):
        newest, every = (jnp.concatenate(half, axis=1) for half in zip(one, two))
        both = both + lax.dot_general(newest, every, NT, preferred_element_type=F32)
    both = both[:R] + both[R:]
    row4 = jnp.concatenate([both[:, :COLS] + both[:, COLS:], jnp.zeros((R, L - COLS), F32)], axis=1)
    row0, row1, row2, row3 = (r[...] for r in rows)
    outs[0][:R, :] = row4 + pltpu.roll(row2, 5 * R, 1)
    outs[0][R:, :] = row3 + pltpu.roll(row1, 4 * R, 1) + pltpu.roll(row0, 6 * R, 1)


def unpacked(g_ref):
    one, two = g_ref[:R, :], g_ref[R:, :]
    shifted = [
        pltpu.roll(two, L - 6 * R, 1),
        pltpu.roll(two, L - 4 * R, 1),
        pltpu.roll(one, L - 5 * R, 1),
        two,
        one,
    ]
    lane = lax.broadcasted_iota(jnp.int32, (R, L), 1)
    rows = [jnp.where(lane < (k + 1) * R, row, 0.0) for k, row in enumerate(shifted)]
    lower = jnp.concatenate(rows + [jnp.zeros((L - COLS, L), F32)], axis=0)
    across = jnp.transpose(lower)
    return [
        jnp.where(lane < (k + 1) * R, rows[k], across[k * R : (k + 1) * R]) for k in range(STEPS + 1)
    ]


def factor(tiles):
    n = len(tiles)
    lane = lax.broadcasted_iota(jnp.int32, (8, L), 1)
    sub = lax.broadcasted_iota(jnp.int32, (8, L), 0)

    def row(value, s):
        return jnp.broadcast_to(value[s : s + 1, :], (8, L))

    triangle, inverse = [], []
    for t in range(n):
        base = 8 * t
        panel = [
            [jnp.broadcast_to(tiles[j][:, base + c : base + c + 1], (8, L)) for c in range(8)]
            for j in range(t, n)
        ]
        inside = jnp.logical_and(lane >= base, lane < base + 8)
        tiles[t] = jnp.where(inside, jnp.where(lane - base == sub, 1.0, 0.0), tiles[t])
        for j in range(t + 1, n):
            tiles[j] = jnp.where(inside, 0.0, tiles[j])
        pivots = None
        for s in range(8):
            pivot = row(panel[0][s], s)
            pivots = pivot if s == 0 else jnp.where(sub == s, pivot, pivots)
            one_over = 1.0 / pivot
            scaled = row(tiles[t], s) * one_over
            ahead = [row(panel[0][c], s) * one_over for c in range(s + 1, 8)]
            for j in range(t, n):
                factors = panel[j - t][s]
                if j == t:
                    factors = jnp.where(sub > s, factors, 0.0)
                for c in range(s + 1, 8):
                    panel[j - t][c] = panel[j - t][c] - factors * ahead[c - s - 1]
                tiles[j] = tiles[j] - factors * scaled
        scale = lax.rsqrt(pivots)
        rows = tiles[t] * scale
        inverse.append(jnp.where(lane < base + 8, rows, 0.0))
        rows = jnp.where(lane < base + 8, 0.0, rows)
        for c in range(8):
            here = jnp.logical_and(lane == base + c, sub <= c)
            rows = jnp.where(here, panel[0][c] * scale, rows)
        triangle.append(rows)
    return triangle, inverse


def finish_kernel(g_ref, *refs):
    count = STEPS + 1
    highs, lows, (q_ref, r_ref) = refs[:count], refs[count : 2 * count], refs[2 * count :]
    tiles = [half for row in unpacked(g_ref) for half in (row[:8], row[8:])]
    triangle, inverse = factor(tiles)
    r_ref[...] = jnp.concatenate(triangle, axis=0)[:, :COLS]
    inverse = jnp.concatenate(inverse, axis=0)[:, :COLS]
    high, low = (half.astype(F32) for half in split(inverse))
    left = jnp.concatenate([high, high, low], axis=1).astype(BF16)
    for x in range(2):
        for z in range(Z):
            here = lanes(x, z)
            high = [h[:, here] for h in highs]
            low = [l[:, here] for l in lows]
            right = jnp.concatenate(high + low + high, axis=0)
            rows = jnp.transpose(jnp.dot(left, right, preferred_element_type=F32))
            q_ref[x, 0, z] = rows[:U]
            q_ref[x, 1, z] = rows[U:]


def call(kernel, outs, operands, **more):
    return pl.pallas_call(
        kernel,
        out_shape=[jax.ShapeDtypeStruct(*s) for s in outs],
        in_specs=more.pop("in_specs", [VM] * len(operands)),
        out_specs=more.pop("out_specs", [VM] * len(outs)),
        compiler_params=pltpu.CompilerParams(vmem_limit_bytes=VMEM_LIMIT),
        **more,
    )(*operands)


BLOCK = ((R, WIDE), F32)
HALVES = [((R, WIDE), BF16)] * 2
PACKETS = [((R, FACE), F32)] * 4
GRAM_ROW = ((R, L), F32)


def exchange(packets):
    wide = lax.axis_size("gx")
    deep = lax.axis_size("gy")

    def even(n):
        return [(i, i ^ 1) for i in range(n)]

    def odd(n):
        there = [(i, (i + 1) % n) for i in range(1, n, 2)]
        return there + [(j, i) for i, j in there]

    e, o, ee, oo = packets
    oo = lax.ppermute(oo, "gy", odd(deep))
    ee = lax.ppermute(ee, "gy", even(deep))
    o = lax.ppermute(o, "gx", odd(wide))
    e = lax.ppermute(e, "gx", even(wide))
    return e, o, ee, oo


GROUPS = ((8, 9, 1), (16 + 8, 48 + 8, 32 + 8), (64 + 8, 192 + 8, 128 + 8), (2 + 8, 6 + 8, 5 + 8))


def total_over_devices(gram):
    axes = ("gx", "gy")
    count = lax.axis_size("gx") * lax.axis_size("gy")
    for masks in GROUPS:
        terms = [lax.ppermute(gram, axes, [(i, i ^ m) for i in range(count)]) for m in masks]
        gram = gram + terms[0]
        if len(masks) == 3:
            gram = gram + (terms[1] + terms[2])
    return gram


def first_product(operator_blocks, high, low):
    return call(
        first_kernel,
        [((2, Z, L, 2 * TILES * L), BF16), ((2, Z, L, 2 * OUTER * L), BF16), BLOCK],
        [pltpu.with_memory_space_constraint(operator_blocks, pltpu.HBM), high, low],
        in_specs=[pl.BlockSpec(memory_space=pltpu.HBM), VM, VM],
        scratch_shapes=[pltpu.VMEM((2, 2, Z, 7, U, U), F32), pltpu.SemaphoreType.DMA((Z,))],
    )


def per_device(operator_blocks, start_block):
    start = jnp.swapaxes(start_block, 3, 4)
    now, high, low, *packets = call(begin_kernel, [BLOCK] + HALVES + PACKETS, [start])
    arrived = exchange(packets)
    local, outer, part = first_product(operator_blocks, high, low)
    recent, highs, lows, rows = [now], [high], [low], []
    for step in range(STEPS):
        last = step == STEPS - 1
        if step > 0:
            part, *new_rows = call(
                functools.partial(local_kernel, step),
                [BLOCK] + [GRAM_ROW] * (2 if step == 1 else 1),
                [local, *highs, *lows],
            )
            rows += new_rows
        high, low, *outs = call(
            functools.partial(outer_kernel, step),
            HALVES + ([((2 * R, L), F32)] if last else [BLOCK] + PACKETS),
            [*recent, *(rows + highs + lows if last else []), part, *arrived, outer],
        )
        highs.append(high)
        lows.append(low)
        if not last:
            recent = [outs[0], recent[0]]
            arrived = exchange(outs[1:])
    gram = total_over_devices(outs[0])
    return call(
        finish_kernel,
        [((2, 2, Z, U, COLS), F32), ((COLS, COLS), F32)],
        [gram, *highs, *lows],
    )


def solution(mesh):
    in_specs = (P("gx", "gy", None, None, None, None), P("gx", "gy", None, None, None))
    out_specs = (P("gx", "gy", None, None, None), P())
    return jax.shard_map(
        per_device, mesh=mesh, in_specs=in_specs, out_specs=out_specs, check_vma=False
    )
```

time: 80.3 us -> 78.2 us (0.974)
  Pallas kernels: 24.7 us -> 22 us
    pallas_call x1 -> x0, Pallas kernels: 6.38 us -> none  [first_product(): pl.pallas_call(first_kernel, out_shape=[jax.ShapeDtypeStruct(*s) for s in...]
    pallas_call x9 -> x10, Pallas kernels: 18.3 us -> 22 us  [call(): pl.pallas_call(kernel, out_shape=[jax.ShapeDtypeStruct(*s) for s in outs]...]
  transfers between devices with their start and end apart: 28 -> 28, of which waited for: 14 -> 14; matrix products, arithmetic and copies ran while one was open for 0% -> 0% of each run, Pallas kernels for 17% -> 16%
where the time goes in v2:
time: 78.2 us; the launch traced here: 78.1 us
  starting transfers between devices  42.3 us (54%)
  Pallas kernels  22 us (28%)
  waiting for transfers between devices  12 us (15%)
  local copies, waits for them, and re-layouts  0.99 us (1%)
    pallas_call x10, Pallas kernels, call(): pl.pallas_call(kernel, out_shape=[jax.ShapeDtypeStruct(*s) for s in outs]...  22 us
    ppermute x12, starting transfers between devices, total_over_devices(): lax.ppermute(gram, axes, [(i, i ^ m) for i in range(count)])  17.3 us
    ppermute x4, starting transfers between devices, exchange(): e = lax.ppermute(e, 'gx', even(wide))  14.4 us
    ppermute x4, starting transfers between devices, exchange(): oo = lax.ppermute(oo, 'gy', odd(deep))  8.77 us
    ppermute x12, waiting for transfers between devices, total_over_devices(): lax.ppermute(gram, axes, [(i, i ^ m) for i in range(count)])  8.73 us
    ppermute x4, waiting for transfers between devices, exchange(): oo = lax.ppermute(oo, 'gy', odd(deep))  1.89 us
    ppermute x4, starting transfers between devices, exchange(): ee = lax.ppermute(ee, 'gy', even(deep))  1.66 us
  transfers between devices with their start and end apart: 28, of which 14 were waited for; matrix products, arithmetic and copies ran while one was open for 0% of the time, Pallas kernels for 16%

profile of v2, /device:TPU:1, one launch (start us, length us, event | category | flops | bytes accessed | tf_op | source)
XLA Modules:
  0.0 78.1 jit_solution(7161530346324162486)
XLA Ops:
  0.6 1.0 %copy-done = f32[2,2,12,64,16]{3,4,2,1,0:T(8,128)S(1)} copy-done((f32[2,2,12,64,16]{3,4,2,1,0:T(8,128)S(1)}, f32[2,2,12,64,16]{3,4,2,1,0:T(8,128)}, u32[]{:S(2)}) %copy-start) | copy-done | bytes 196632
  1.6 0.2 shard_map.41
  1.8 3.3 %collective-permute-start = (f32[16,1536]{1,0:T(8,128)S(1)}, f32[16,1536]{1,0:T(8,128)S(1)}, u32[]{:S(2)}, u32[]{:S(2)}) collective-permute-start(f32[16,1536]{1,0:T(8,128)S(1)} %get-tuple-element.47), channel_id=1, source_target_pairs={{0,8},{8,0},{16,24},{24,16},{32,40},{40,32},{48,56},{56,48},{64,72... | collective-permute-start | bytes 294920 | tf_op jit(solution)/shard_map/ppermute | solution.py:344
  5.1 0.0 collective-permute-start.1
  5.1 1.1 %collective-permute-start.2 = (f32[16,1536]{1,0:T(8,128)S(1)}, f32[16,1536]{1,0:T(8,128)S(1)}, u32[]{:S(2)}, u32[]{:S(2)}) collective-permute-start(f32[16,1536]{1,0:T(8,128)S(1)} %get-tuple-element.49), channel_id=1, source_target_pairs={{0,1},{1,0},{2,3},{3,2},{4,5},{5,4},{6,7},{7,6},{8,9},{9,8},{10,11... | collective-permute-start | bytes 294920 | tf_op jit(solution)/shard_map/ppermute | solution.py:342
  6.2 4.7 %collective-permute-start.3 = (f32[16,1536]{1,0:T(8,128)S(1)}, f32[16,1536]{1,0:T(8,128)S(1)}, u32[]{:S(2)}, u32[]{:S(2)}) collective-permute-start(f32[16,1536]{1,0:T(8,128)S(1)} %get-tuple-element.50), channel_id=1, source_target_pairs={{1,2},{3,4},{5,6},{7,0},{2,1},{4,3},{6,5},{0,7},{9,10},{11,12},{13... | collective-permute-start | bytes 294920 | tf_op jit(solution)/shard_map/ppermute | solution.py:341
  10.9 5.7 %shard_map.42 = (bf16[2,12,128,1024]{3,2,1,0:T(8,128)(2,1)S(1)}, bf16[2,12,128,512]{3,2,1,0:T(8,128)(2,1)S(1)}, f32[16,3072]{1,0:T(8,128)S(1)}) custom-call(f32[2,2,12,7,64,64]{5,4,3,2,1,0:T(8,128)} %a_ref.1, bf16[16,3072]{1,0:T(8,128)(2,1)S(1)} %get-tuple-element.44.h_ref.refs_0_.refs_6_, ...), custom_call_target="tpu_custom_call" | custom-call | tf_op jit(solution)/shard_map/pallas_call | solution.py:313
  16.6 1.2 %shard_map.43 = (bf16[16,3072]{1,0:T(8,128)(2,1)S(1)}, bf16[16,3072]{1,0:T(8,128)(2,1)S(1)}, f32[16,3072]{1,0:T(8,128)S(1)}, f32[16,1536]{1,0:T(8,128)S(1)}, f32...) custom-call(f32[16,3072]{1,0:T(8,128)S(1)} %get-tuple-element.43.refs_0_.refs_1_, ...), custom_call_target="tpu_custom_call" | custom-call | tf_op jit(solution)/shard_map/pallas_call | solution.py:313
  17.8 4.8 %collective-permute-start.4 = (f32[16,1536]{1,0:T(8,128)S(1)}, f32[16,1536]{1,0:T(8,128)S(1)}, u32[]{:S(2)}, u32[]{:S(2)}) collective-permute-start(f32[16,1536]{1,0:T(8,128)S(1)} %get-tuple-element.57), channel_id=1, source_target_pairs={{0,8},{8,0},{16,24},{24,16},{32,40},{40,32},{48,56},{56,48},{64,72... | collective-permute-start | bytes 294920 | tf_op jit(solution)/shard_map/ppermute | solution.py:344
  22.6 1.5 %collective-permute-start.7 = (f32[16,1536]{1,0:T(8,128)S(1)}, f32[16,1536]{1,0:T(8,128)S(1)}, u32[]{:S(2)}, u32[]{:S(2)}) collective-permute-start(f32[16,1536]{1,0:T(8,128)S(1)} %get-tuple-element.60), channel_id=1, source_target_pairs={{1,2},{3,4},{5,6},{7,0},{2,1},{4,3},{6,5},{0,7},{9,10},{11,12},{13... | collective-permute-start | bytes 294920 | tf_op jit(solution)/shard_map/ppermute | solution.py:341
  24.0 2.2 %shard_map.44 = (f32[16,3072]{1,0:T(8,128)S(1)}, f32[16,128]{1,0:T(8,128)S(1)}, f32[16,128]{1,0:T(8,128)S(1)}) custom-call(bf16[2,12,128,1024]{3,2,1,0:T(8,128)(2,1)S(1)} %get-tuple-element.53.w_ref, bf16[16,3072]{1,0:T(8,128)(2,1)S(1)} %get-tuple-element.44.h_ref.refs_0_.refs_6_, bf16[16,3072]{1,0:T(8,128)(2,1)S(1)} %get-tuple-element.54.refs_1_.refs_7_, ...), custom_call_target="tpu_custom_call" | custom-call | tf_op jit(solution)/shard_map/pallas_call | solution.py:313
  26.3 0.6 collective-permute-done.5.refs_4_
  26.9 0.3 collective-permute-done.7.refs_6_
  27.3 1.2 %shard_map.45 = (bf16[16,3072]{1,0:T(8,128)(2,1)S(1)}, bf16[16,3072]{1,0:T(8,128)(2,1)S(1)}, f32[16,3072]{1,0:T(8,128)S(1)}, f32[16,1536]{1,0:T(8,128)S(1)}, f32...) custom-call(f32[16,3072]{1,0:T(8,128)S(1)} %get-tuple-element.52.refs_0_.refs_1_, ...), custom_call_target="tpu_custom_call" | custom-call | tf_op jit(solution)/shard_map/pallas_call | solution.py:313
  28.5 2.9 %collective-permute-start.8 = (f32[16,1536]{1,0:T(8,128)S(1)}, f32[16,1536]{1,0:T(8,128)S(1)}, u32[]{:S(2)}, u32[]{:S(2)}) collective-permute-start(f32[16,1536]{1,0:T(8,128)S(1)} %get-tuple-element.65), channel_id=1, source_target_pairs={{0,8},{8,0},{16,24},{24,16},{32,40},{40,32},{48,56},{56,48},{64,72... | collective-permute-start | bytes 294920 | tf_op jit(solution)/shard_map/ppermute | solution.py:344
  31.3 0.2 collective-permute-start.9
  31.5 0.5 collective-permute-start.10
  32.1 1.2 %collective-permute-start.11 = (f32[16,1536]{1,0:T(8,128)S(1)}, f32[16,1536]{1,0:T(8,128)S(1)}, u32[]{:S(2)}, u32[]{:S(2)}) collective-permute-start(f32[16,1536]{1,0:T(8,128)S(1)} %get-tuple-element.68), channel_id=1, source_target_pairs={{1,2},{3,4},{5,6},{7,0},{2,1},{4,3},{6,5},{0,7},{9,10},{11,12},{13... | collective-permute-start | bytes 294920 | tf_op jit(solution)/shard_map/ppermute | solution.py:341
  33.3 2.2 %shard_map.46 = (f32[16,3072]{1,0:T(8,128)S(1)}, f32[16,128]{1,0:T(8,128)S(1)}) custom-call(bf16[2,12,128,1024]{3,2,1,0:T(8,128)(2,1)S(1)} %get-tuple-element.53.w_ref, bf16[16,3072]{1,0:T(8,128)(2,1)S(1)} %get-tuple-element.44.h_ref.refs_0_.refs_6_, bf16[16,3072]{1,0:T(8,128)(2,1)S(1)} %get-tuple-element.54.refs_1_.refs_7_, ...), custom_call_target="tpu_custom_call" | custom-call | tf_op jit(solution)/shard_map/pallas_call | solution.py:313
  35.5 0.0 collective-permute-done.10.refs_5_
  35.5 1.2 %collective-permute-done.11.refs_6_ = f32[16,1536]{1,0:T(8,128)S(1)} collective-permute-done((f32[16,1536]{1,0:T(8,128)S(1)}, f32[16,1536]{1,0:T(8,128)S(1)}, u32[]{:S(2)}, u32[]{:S(2)}) %collective-permute-start.11) | collective-permute-done | bytes 98336 | tf_op jit(solution)/shard_map/ppermute | solution.py:341
  36.7 1.2 %shard_map.47 = (bf16[16,3072]{1,0:T(8,128)(2,1)S(1)}, bf16[16,3072]{1,0:T(8,128)(2,1)S(1)}, f32[16,3072]{1,0:T(8,128)S(1)}, f32[16,1536]{1,0:T(8,128)S(1)}, f32...) custom-call(f32[16,3072]{1,0:T(8,128)S(1)} %get-tuple-element.61.refs_0_.refs_1_, ...), custom_call_target="tpu_custom_call" | custom-call | tf_op jit(solution)/shard_map/pallas_call | solution.py:313
  38.0 3.5 %collective-permute-start.12 = (f32[16,1536]{1,0:T(8,128)S(1)}, f32[16,1536]{1,0:T(8,128)S(1)}, u32[]{:S(2)}, u32[]{:S(2)}) collective-permute-start(f32[16,1536]{1,0:T(8,128)S(1)} %get-tuple-element.77), channel_id=1, source_target_pairs={{0,8},{8,0},{16,24},{24,16},{32,40},{40,32},{48,56},{56,48},{64,72... | collective-permute-start | bytes 294920 | tf_op jit(solution)/shard_map/ppermute | solution.py:344
  41.4 1.4 %collective-permute-start.15 = (f32[16,1536]{1,0:T(8,128)S(1)}, f32[16,1536]{1,0:T(8,128)S(1)}, u32[]{:S(2)}, u32[]{:S(2)}) collective-permute-start(f32[16,1536]{1,0:T(8,128)S(1)} %get-tuple-element.80), channel_id=1, source_target_pairs={{1,2},{3,4},{5,6},{7,0},{2,1},{4,3},{6,5},{0,7},{9,10},{11,12},{13... | collective-permute-start | bytes 294920 | tf_op jit(solution)/shard_map/ppermute | solution.py:341
  42.9 2.2 %shard_map.48 = (f32[16,3072]{1,0:T(8,128)S(1)}, f32[16,128]{1,0:T(8,128)S(1)}) custom-call(bf16[2,12,128,1024]{3,2,1,0:T(8,128)(2,1)S(1)} %get-tuple-element.53.w_ref, bf16[16,3072]{1,0:T(8,128)(2,1)S(1)} %get-tuple-element.44.h_ref.refs_0_.refs_6_, bf16[16,3072]{1,0:T(8,128)(2,1)S(1)} %get-tuple-element.54.refs_1_.refs_7_, ...), custom_call_target="tpu_custom_call" | custom-call | tf_op jit(solution)/shard_map/pallas_call | solution.py:313
  45.1 0.7 collective-permute-done.13.refs_16_
  45.8 0.3 collective-permute-done.15.refs_18_
  46.1 1.5 %shard_map.49 = (bf16[16,3072]{1,0:T(8,128)(2,1)S(1)}, bf16[16,3072]{1,0:T(8,128)(2,1)S(1)}, f32[32,128]{1,0:T(8,128)S(1)}) custom-call(f32[16,3072]{1,0:T(8,128)S(1)} %get-tuple-element.69.refs_0_, f32[16,3072]{1,0:T(8,128)S(1)} %get-tuple-element.61.refs_0_.refs_1_, f32[16,128]{1,0:T(8,128)S(1)} %get-tuple-element.70.refs_2_, ...), custom_call_target="tpu_custom_call" | custom-call | tf_op jit(solution)/shard_map/pallas_call | solution.py:313
  47.6 0.6 collective-permute-start.18
  48.3 3.9 %collective-permute-start.17 = (f32[32,128]{1,0:T(8,128)S(1)}, f32[32,128]{1,0:T(8,128)S(1)}, u32[]{:S(2)}, u32[]{:S(2)}) collective-permute-start(f32[32,128]{1,0:T(8,128)S(1)} %get-tuple-element.81), channel_id=1, source_target_pairs={{0,9},{1,8},{2,11},{3,10},{4,13},{5,12},{6,15},{7,14},{8,1},{9,0},... | collective-permute-start | bytes 49160 | tf_op jit(solution)/shard_map/ppermute | solution.py:355
  52.1 1.7 %collective-permute-done.17 = f32[32,128]{1,0:T(8,128)S(1)} collective-permute-done((f32[32,128]{1,0:T(8,128)S(1)}, f32[32,128]{1,0:T(8,128)S(1)}, u32[]{:S(2)}, u32[]{:S(2)}) %collective-permute-start.17) | collective-permute-done | bytes 16416 | tf_op jit(solution)/shard_map/ppermute | solution.py:355
  53.9 0.6 collective-permute-start.21
  54.4 2.8 %collective-permute-start.20 = (f32[32,128]{1,0:T(8,128)S(1)}, f32[32,128]{1,0:T(8,128)S(1)}, u32[]{:S(2)}, u32[]{:S(2)}) collective-permute-start(f32[32,128]{1,0:T(8,128)S(1)} %add_add_fusion.3), channel_id=1, source_target_pairs={{0,56},{1,57},{2,58},{3,59},{4,60},{5,61},{6,62},{7,63},{8,48},{9,... | collective-permute-start | bytes 49160 | tf_op jit(solution)/shard_map/ppermute | solution.py:355
  57.3 1.4 %collective-permute-done.21 = f32[32,128]{1,0:T(8,128)S(1)} collective-permute-done((f32[32,128]{1,0:T(8,128)S(1)}, f32[32,128]{1,0:T(8,128)S(1)}, u32[]{:S(2)}, u32[]{:S(2)}) %collective-permute-start.21) | collective-permute-done | bytes 16416 | tf_op jit(solution)/shard_map/ppermute | solution.py:355
  58.6 0.4 collective-permute-done.20
  59.0 1.4 %collective-permute-done.19 = f32[32,128]{1,0:T(8,128)S(1)} collective-permute-done((f32[32,128]{1,0:T(8,128)S(1)}, f32[32,128]{1,0:T(8,128)S(1)}, u32[]{:S(2)}, u32[]{:S(2)}) %collective-permute-start.19) | collective-permute-done | bytes 16416 | tf_op jit(solution)/shard_map/ppermute | solution.py:355
  60.4 0.1 collective-permute-start.24
  60.5 0.2 collective-permute-start.23
  60.7 3.0 %collective-permute-start.22 = (f32[32,128]{1,0:T(8,128)S(1)}, f32[32,128]{1,0:T(8,128)S(1)}, u32[]{:S(2)}, u32[]{:S(2)}) collective-permute-start(f32[32,128]{1,0:T(8,128)S(1)} %add_add_fusion.2), channel_id=1, source_target_pairs={{0,72},{1,73},{2,74},{3,75},{4,76},{5,77},{6,78},{7,79},{8,64},{9,... | collective-permute-start | bytes 49160 | tf_op jit(solution)/shard_map/ppermute | solution.py:355
  63.7 1.5 %collective-permute-done.24 = f32[32,128]{1,0:T(8,128)S(1)} collective-permute-done((f32[32,128]{1,0:T(8,128)S(1)}, f32[32,128]{1,0:T(8,128)S(1)}, u32[]{:S(2)}, u32[]{:S(2)}) %collective-permute-start.24) | collective-permute-done | bytes 16416 | tf_op jit(solution)/shard_map/ppermute | solution.py:355
  65.2 0.1 collective-permute-done.23
  65.3 3.0 %collective-permute-start.27 = (f32[32,128]{1,0:T(8,128)S(1)}, f32[32,128]{1,0:T(8,128)S(1)}, u32[]{:S(2)}, u32[]{:S(2)}) collective-permute-start(f32[32,128]{1,0:T(8,128)S(1)} %add_add_fusion.1), channel_id=1, source_target_pairs={{0,13},{1,12},{2,15},{3,14},{4,9},{5,8},{6,11},{7,10},{8,5},{9,4},... | collective-permute-start | bytes 49160 | tf_op jit(solution)/shard_map/ppermute | solution.py:355
  68.2 1.4 %collective-permute-start.26 = (f32[32,128]{1,0:T(8,128)S(1)}, f32[32,128]{1,0:T(8,128)S(1)}, u32[]{:S(2)}, u32[]{:S(2)}) collective-permute-start(f32[32,128]{1,0:T(8,128)S(1)} %add_add_fusion.1), channel_id=1, source_target_pairs={{0,14},{1,15},{2,12},{3,13},{4,10},{5,11},{6,8},{7,9},{8,6},{9,7},... | collective-permute-start | bytes 49160 | tf_op jit(solution)/shard_map/ppermute | solution.py:355
  69.6 1.7 %collective-permute-start.25 = (f32[32,128]{1,0:T(8,128)S(1)}, f32[32,128]{1,0:T(8,128)S(1)}, u32[]{:S(2)}, u32[]{:S(2)}) collective-permute-start(f32[32,128]{1,0:T(8,128)S(1)} %add_add_fusion.1), channel_id=1, source_target_pairs={{0,10},{1,11},{2,8},{3,9},{4,14},{5,15},{6,12},{7,13},{8,2},{9,3},... | collective-permute-start | bytes 49160 | tf_op jit(solution)/shard_map/ppermute | solution.py:355
  71.4 0.2 collective-permute-done.27
  71.5 2.0 %collective-permute-done.26 = f32[32,128]{1,0:T(8,128)S(1)} collective-permute-done((f32[32,128]{1,0:T(8,128)S(1)}, f32[32,128]{1,0:T(8,128)S(1)}, u32[]{:S(2)}, u32[]{:S(2)}) %collective-permute-start.26) | collective-permute-done | bytes 16416 | tf_op jit(solution)/shard_map/ppermute | solution.py:355
  73.5 0.2 collective-permute-done.25
  73.7 4.3 %shard_map.50 = (f32[2,2,12,64,80]{4,3,2,1,0:T(8,128)}, f32[80,80]{1,0:T(8,128)}) custom-call(f32[32,128]{1,0:T(8,128)S(1)} %add_add_fusion.g_ref, bf16[16,3072]{1,0:T(8,128)(2,1)S(1)} %get-tuple-element.44.h_ref.refs_0_.refs_6_, bf16[16,3072]{1,0:T(8,128)(2,1)S(1)} %get-tuple-element.54.refs_1_.refs_7_, ...), custom_call_target="tpu_custom_call" | custom-call | tf_op jit(solution)/shard_map/pallas_call | solution.py:313
  (24 shorter events, 0.1 us)
Async XLA Ops:
  0.6 1.0 %copy-start = (f32[2,2,12,64,16]{3,4,2,1,0:T(8,128)S(1)}, f32[2,2,12,64,16]{3,4,2,1,0:T(8,128)}, u32[]{:S(2)}) copy-start(f32[2,2,12,64,16]{3,4,2,1,0:T(8,128)} %param.3) | copy-start | bytes 589828
  1.8 14.8 %collective-permute-start = (f32[16,1536]{1,0:T(8,128)S(1)}, f32[16,1536]{1,0:T(8,128)S(1)}, u32[]{:S(2)}, u32[]{:S(2)}) collective-permute-start(f32[16,1536]{1,0:T(8,128)S(1)} %get-tuple-element.47), channel_id=1, source_target_pairs={{0,8},{8,0},{16,24},{24,16},{32,40},{40,32},{48,56},{56,48},{64,72... | collective-permute-start | bytes 294920 | tf_op jit(solution)/shard_map/ppermute | solution.py:344
  5.1 11.5 %collective-permute-start.1 = (f32[16,1536]{1,0:T(8,128)S(1)}, f32[16,1536]{1,0:T(8,128)S(1)}, u32[]{:S(2)}, u32[]{:S(2)}) collective-permute-start(f32[16,1536]{1,0:T(8,128)S(1)} %get-tuple-element.48), channel_id=1, source_target_pairs={{8,16},{24,32},{40,48},{56,64},{72,80},{88,96},{104,112},{120,128}... | collective-permute-start | bytes 294920 | tf_op jit(solution)/shard_map/ppermute | solution.py:343
  5.1 11.5 %collective-permute-start.2 = (f32[16,1536]{1,0:T(8,128)S(1)}, f32[16,1536]{1,0:T(8,128)S(1)}, u32[]{:S(2)}, u32[]{:S(2)}) collective-permute-start(f32[16,1536]{1,0:T(8,128)S(1)} %get-tuple-element.49), channel_id=1, source_target_pairs={{0,1},{1,0},{2,3},{3,2},{4,5},{5,4},{6,7},{7,6},{8,9},{9,8},{10,11... | collective-permute-start | bytes 294920 | tf_op jit(solution)/shard_map/ppermute | solution.py:342
  6.2 10.4 %collective-permute-start.3 = (f32[16,1536]{1,0:T(8,128)S(1)}, f32[16,1536]{1,0:T(8,128)S(1)}, u32[]{:S(2)}, u32[]{:S(2)}) collective-permute-start(f32[16,1536]{1,0:T(8,128)S(1)} %get-tuple-element.50), channel_id=1, source_target_pairs={{1,2},{3,4},{5,6},{7,0},{2,1},{4,3},{6,5},{0,7},{9,10},{11,12},{13... | collective-permute-start | bytes 294920 | tf_op jit(solution)/shard_map/ppermute | solution.py:341
  17.8 8.5 %collective-permute-start.4 = (f32[16,1536]{1,0:T(8,128)S(1)}, f32[16,1536]{1,0:T(8,128)S(1)}, u32[]{:S(2)}, u32[]{:S(2)}) collective-permute-start(f32[16,1536]{1,0:T(8,128)S(1)} %get-tuple-element.57), channel_id=1, source_target_pairs={{0,8},{8,0},{16,24},{24,16},{32,40},{40,32},{48,56},{56,48},{64,72... | collective-permute-start | bytes 294920 | tf_op jit(solution)/shard_map/ppermute | solution.py:344
  22.6 4.3 %collective-permute-start.5 = (f32[16,1536]{1,0:T(8,128)S(1)}, f32[16,1536]{1,0:T(8,128)S(1)}, u32[]{:S(2)}, u32[]{:S(2)}) collective-permute-start(f32[16,1536]{1,0:T(8,128)S(1)} %get-tuple-element.58), channel_id=1, source_target_pairs={{8,16},{24,32},{40,48},{56,64},{72,80},{88,96},{104,112},{120,128}... | collective-permute-start | bytes 294920 | tf_op jit(solution)/shard_map/ppermute | solution.py:343
  22.6 4.3 %collective-permute-start.6 = (f32[16,1536]{1,0:T(8,128)S(1)}, f32[16,1536]{1,0:T(8,128)S(1)}, u32[]{:S(2)}, u32[]{:S(2)}) collective-permute-start(f32[16,1536]{1,0:T(8,128)S(1)} %get-tuple-element.59), channel_id=1, source_target_pairs={{0,1},{1,0},{2,3},{3,2},{4,5},{5,4},{6,7},{7,6},{8,9},{9,8},{10,11... | collective-permute-start | bytes 294920 | tf_op jit(solution)/shard_map/ppermute | solution.py:342
  22.6 4.7 %collective-permute-start.7 = (f32[16,1536]{1,0:T(8,128)S(1)}, f32[16,1536]{1,0:T(8,128)S(1)}, u32[]{:S(2)}, u32[]{:S(2)}) collective-permute-start(f32[16,1536]{1,0:T(8,128)S(1)} %get-tuple-element.60), channel_id=1, source_target_pairs={{1,2},{3,4},{5,6},{7,0},{2,1},{4,3},{6,5},{0,7},{9,10},{11,12},{13... | collective-permute-start | bytes 294920 | tf_op jit(solution)/shard_map/ppermute | solution.py:341
  28.5 7.0 %collective-permute-start.8 = (f32[16,1536]{1,0:T(8,128)S(1)}, f32[16,1536]{1,0:T(8,128)S(1)}, u32[]{:S(2)}, u32[]{:S(2)}) collective-permute-start(f32[16,1536]{1,0:T(8,128)S(1)} %get-tuple-element.65), channel_id=1, source_target_pairs={{0,8},{8,0},{16,24},{24,16},{32,40},{40,32},{48,56},{56,48},{64,72... | collective-permute-start | bytes 294920 | tf_op jit(solution)/shard_map/ppermute | solution.py:344
  31.3 4.2 %collective-permute-start.9 = (f32[16,1536]{1,0:T(8,128)S(1)}, f32[16,1536]{1,0:T(8,128)S(1)}, u32[]{:S(2)}, u32[]{:S(2)}) collective-permute-start(f32[16,1536]{1,0:T(8,128)S(1)} %get-tuple-element.66), channel_id=1, source_target_pairs={{8,16},{24,32},{40,48},{56,64},{72,80},{88,96},{104,112},{120,128}... | collective-permute-start | bytes 294920 | tf_op jit(solution)/shard_map/ppermute | solution.py:343
  31.5 4.0 %collective-permute-start.10 = (f32[16,1536]{1,0:T(8,128)S(1)}, f32[16,1536]{1,0:T(8,128)S(1)}, u32[]{:S(2)}, u32[]{:S(2)}) collective-permute-start(f32[16,1536]{1,0:T(8,128)S(1)} %get-tuple-element.67), channel_id=1, source_target_pairs={{0,1},{1,0},{2,3},{3,2},{4,5},{5,4},{6,7},{7,6},{8,9},{9,8},{10,11... | collective-permute-start | bytes 294920 | tf_op jit(solution)/shard_map/ppermute | solution.py:342
  32.1 4.7 %collective-permute-start.11 = (f32[16,1536]{1,0:T(8,128)S(1)}, f32[16,1536]{1,0:T(8,128)S(1)}, u32[]{:S(2)}, u32[]{:S(2)}) collective-permute-start(f32[16,1536]{1,0:T(8,128)S(1)} %get-tuple-element.68), channel_id=1, source_target_pairs={{1,2},{3,4},{5,6},{7,0},{2,1},{4,3},{6,5},{0,7},{9,10},{11,12},{13... | collective-permute-start | bytes 294920 | tf_op jit(solution)/shard_map/ppermute | solution.py:341
  38.0 7.1 %collective-permute-start.12 = (f32[16,1536]{1,0:T(8,128)S(1)}, f32[16,1536]{1,0:T(8,128)S(1)}, u32[]{:S(2)}, u32[]{:S(2)}) collective-permute-start(f32[16,1536]{1,0:T(8,128)S(1)} %get-tuple-element.77), channel_id=1, source_target_pairs={{0,8},{8,0},{16,24},{24,16},{32,40},{40,32},{48,56},{56,48},{64,72... | collective-permute-start | bytes 294920 | tf_op jit(solution)/shard_map/ppermute | solution.py:344
  41.4 4.3 %collective-permute-start.13 = (f32[16,1536]{1,0:T(8,128)S(1)}, f32[16,1536]{1,0:T(8,128)S(1)}, u32[]{:S(2)}, u32[]{:S(2)}) collective-permute-start(f32[16,1536]{1,0:T(8,128)S(1)} %get-tuple-element.78), channel_id=1, source_target_pairs={{8,16},{24,32},{40,48},{56,64},{72,80},{88,96},{104,112},{120,128}... | collective-permute-start | bytes 294920 | tf_op jit(solution)/shard_map/ppermute | solution.py:343
  41.4 4.3 %collective-permute-start.14 = (f32[16,1536]{1,0:T(8,128)S(1)}, f32[16,1536]{1,0:T(8,128)S(1)}, u32[]{:S(2)}, u32[]{:S(2)}) collective-permute-start(f32[16,1536]{1,0:T(8,128)S(1)} %get-tuple-element.79), channel_id=1, source_target_pairs={{0,1},{1,0},{2,3},{3,2},{4,5},{5,4},{6,7},{7,6},{8,9},{9,8},{10,11... | collective-permute-start | bytes 294920 | tf_op jit(solution)/shard_map/ppermute | solution.py:342
  41.4 4.7 %collective-permute-start.15 = (f32[16,1536]{1,0:T(8,128)S(1)}, f32[16,1536]{1,0:T(8,128)S(1)}, u32[]{:S(2)}, u32[]{:S(2)}) collective-permute-start(f32[16,1536]{1,0:T(8,128)S(1)} %get-tuple-element.80), channel_id=1, source_target_pairs={{1,2},{3,4},{5,6},{7,0},{2,1},{4,3},{6,5},{0,7},{9,10},{11,12},{13... | collective-permute-start | bytes 294920 | tf_op jit(solution)/shard_map/ppermute | solution.py:341
  47.6 4.5 %collective-permute-start.18 = (f32[32,128]{1,0:T(8,128)S(1)}, f32[32,128]{1,0:T(8,128)S(1)}, u32[]{:S(2)}, u32[]{:S(2)}) collective-permute-start(f32[32,128]{1,0:T(8,128)S(1)} %get-tuple-element.81), channel_id=1, source_target_pairs={{0,1},{1,0},{2,3},{3,2},{4,5},{5,4},{6,7},{7,6},{8,9},{9,8},{10,11... | collective-permute-start | bytes 49160 | tf_op jit(solution)/shard_map/ppermute | solution.py:355
  48.3 5.6 %collective-permute-start.17 = (f32[32,128]{1,0:T(8,128)S(1)}, f32[32,128]{1,0:T(8,128)S(1)}, u32[]{:S(2)}, u32[]{:S(2)}) collective-permute-start(f32[32,128]{1,0:T(8,128)S(1)} %get-tuple-element.81), channel_id=1, source_target_pairs={{0,9},{1,8},{2,11},{3,10},{4,13},{5,12},{6,15},{7,14},{8,1},{9,0},... | collective-permute-start | bytes 49160 | tf_op jit(solution)/shard_map/ppermute | solution.py:355
  52.1 1.7 %collective-permute-start.16 = (f32[32,128]{1,0:T(8,128)S(1)}, f32[32,128]{1,0:T(8,128)S(1)}, u32[]{:S(2)}, u32[]{:S(2)}) collective-permute-start(f32[32,128]{1,0:T(8,128)S(1)} %get-tuple-element.81), channel_id=1, source_target_pairs={{0,8},{1,9},{2,10},{3,11},{4,12},{5,13},{6,14},{7,15},{8,0},{9,1},... | collective-permute-start | bytes 49160 | tf_op jit(solution)/shard_map/ppermute | solution.py:355
  53.9 4.8 %collective-permute-start.21 = (f32[32,128]{1,0:T(8,128)S(1)}, f32[32,128]{1,0:T(8,128)S(1)}, u32[]{:S(2)}, u32[]{:S(2)}) collective-permute-start(f32[32,128]{1,0:T(8,128)S(1)} %add_add_fusion.3), channel_id=1, source_target_pairs={{0,40},{1,41},{2,42},{3,43},{4,44},{5,45},{6,46},{7,47},{8,32},{9,... | collective-permute-start | bytes 49160 | tf_op jit(solution)/shard_map/ppermute | solution.py:355
  54.4 4.6 %collective-permute-start.20 = (f32[32,128]{1,0:T(8,128)S(1)}, f32[32,128]{1,0:T(8,128)S(1)}, u32[]{:S(2)}, u32[]{:S(2)}) collective-permute-start(f32[32,128]{1,0:T(8,128)S(1)} %add_add_fusion.3), channel_id=1, source_target_pairs={{0,56},{1,57},{2,58},{3,59},{4,60},{5,61},{6,62},{7,63},{8,48},{9,... | collective-permute-start | bytes 49160 | tf_op jit(solution)/shard_map/ppermute | solution.py:355
  57.3 3.2 %collective-permute-start.19 = (f32[32,128]{1,0:T(8,128)S(1)}, f32[32,128]{1,0:T(8,128)S(1)}, u32[]{:S(2)}, u32[]{:S(2)}) collective-permute-start(f32[32,128]{1,0:T(8,128)S(1)} %add_add_fusion.3), channel_id=1, source_target_pairs={{0,24},{1,25},{2,26},{3,27},{4,28},{5,29},{6,30},{7,31},{8,16},{9,... | collective-permute-start | bytes 49160 | tf_op jit(solution)/shard_map/ppermute | solution.py:355
  60.4 4.8 %collective-permute-start.24 = (f32[32,128]{1,0:T(8,128)S(1)}, f32[32,128]{1,0:T(8,128)S(1)}, u32[]{:S(2)}, u32[]{:S(2)}) collective-permute-start(f32[32,128]{1,0:T(8,128)S(1)} %add_add_fusion.2), channel_id=1, source_target_pairs={{0,136},{1,137},{2,138},{3,139},{4,140},{5,141},{6,142},{7,143},{8... | collective-permute-start | bytes 49160 | tf_op jit(solution)/shard_map/ppermute | solution.py:355
  60.5 4.7 %collective-permute-start.23 = (f32[32,128]{1,0:T(8,128)S(1)}, f32[32,128]{1,0:T(8,128)S(1)}, u32[]{:S(2)}, u32[]{:S(2)}) collective-permute-start(f32[32,128]{1,0:T(8,128)S(1)} %add_add_fusion.2), channel_id=1, source_target_pairs={{0,200},{1,201},{2,202},{3,203},{4,204},{5,205},{6,206},{7,207},{8... | collective-permute-start | bytes 49160 | tf_op jit(solution)/shard_map/ppermute | solution.py:355
  60.7 4.5 %collective-permute-start.22 = (f32[32,128]{1,0:T(8,128)S(1)}, f32[32,128]{1,0:T(8,128)S(1)}, u32[]{:S(2)}, u32[]{:S(2)}) collective-permute-start(f32[32,128]{1,0:T(8,128)S(1)} %add_add_fusion.2), channel_id=1, source_target_pairs={{0,72},{1,73},{2,74},{3,75},{4,76},{5,77},{6,78},{7,79},{8,64},{9,... | collective-permute-start | bytes 49160 | tf_op jit(solution)/shard_map/ppermute | solution.py:355
  65.3 6.3 %collective-permute-start.27 = (f32[32,128]{1,0:T(8,128)S(1)}, f32[32,128]{1,0:T(8,128)S(1)}, u32[]{:S(2)}, u32[]{:S(2)}) collective-permute-start(f32[32,128]{1,0:T(8,128)S(1)} %add_add_fusion.1), channel_id=1, source_target_pairs={{0,13},{1,12},{2,15},{3,14},{4,9},{5,8},{6,11},{7,10},{8,5},{9,4},... | collective-permute-start | bytes 49160 | tf_op jit(solution)/shard_map/ppermute | solution.py:355
  68.2 5.3 %collective-permute-start.26 = (f32[32,128]{1,0:T(8,128)S(1)}, f32[32,128]{1,0:T(8,128)S(1)}, u32[]{:S(2)}, u32[]{:S(2)}) collective-permute-start(f32[32,128]{1,0:T(8,128)S(1)} %add_add_fusion.1), channel_id=1, source_target_pairs={{0,14},{1,15},{2,12},{3,13},{4,10},{5,11},{6,8},{7,9},{8,6},{9,7},... | collective-permute-start | bytes 49160 | tf_op jit(solution)/shard_map/ppermute | solution.py:355
  69.6 4.1 %collective-permute-start.25 = (f32[32,128]{1,0:T(8,128)S(1)}, f32[32,128]{1,0:T(8,128)S(1)}, u32[]{:S(2)}, u32[]{:S(2)}) collective-permute-start(f32[32,128]{1,0:T(8,128)S(1)} %add_add_fusion.1), channel_id=1, source_target_pairs={{0,10},{1,11},{2,8},{3,9},{4,14},{5,15},{6,12},{7,13},{8,2},{9,3},... | collective-permute-start | bytes 49160 | tf_op jit(solution)/shard_map/ppermute | solution.py:355
